TPU v7x, 1024 devices: a whole 8x8x8 slice. The times are simulated.
1024 devices in a mesh: half: 2 (over x_hi), ex: 16 (over z, core), fr: 32 (over x_lo, y).
Axes of the slice: x: 8 (x_hi: 2, x_lo: 4; x = x_hi * 4 + x_lo), y: 8, z: 8, core: 2. Of those that a mesh axis runs over, the one named last changes fastest.
Arguments:
- frame_patch_tokens: bfloat16 [2, 32, 32, 256, 1024], P('half', 'fr', 'ex'), may hold values from -12 to 12
- episode_first_frame: int32 [2, 1024], P('half'), may hold values from 0 to 1023, as said below
- router: bfloat16 [1024, 256], replicated, may hold values from -2 to 2
- expert_up_weight: bfloat16 [16, 1024, 2048], P('ex', None, 'half'), may hold values from -0.1875 to 0.1875
- expert_down_weight: bfloat16 [16, 2048, 1024], P('ex', 'half'), may hold values from -0.125 to 0.125
- query_key_value_weight: bfloat16 [1024, 1536], replicated, may hold values from -0.1875 to 0.1875
- head_score_scale: float32 [8], replicated, may hold values from 0.5 to 2
Outputs:
- attended: bfloat16 [2, 1024, 256, 512], P('half', 'fr', 'ex')
Inputs may be any that keep to these rules, and one draw needn't show every extreme that they name: `episode_first_frame`: entry t of a sequence is the first frame of frame t's episode: at most t, equal to t or to entry t - 1, and 0 at t = 0; a new episode begins at the last frame.
All inputs are finite; a program needn't handle non-finite values.
Results may differ from a plain program's by a relative error of at most 0.0088.
Values may be sent and summed in bfloat16 or wider, within the bound.
A program may use at most 64 MiB of HBM per device.

v0:
```python
import functools
import math

import jax
import jax.numpy as jnp
from jax import lax
from jax.experimental import pallas as pl
from jax.experimental.pallas import tpu as pltpu
from jax.sharding import PartitionSpec as P

SPE = 2
HEAD_SIZE = 64
HEADS = 8
WIDTH = HEADS * HEAD_SIZE
NY = 8
WINDOW = 128
MESH = pl.DeviceIdType.MESH

epsilon = 1e-06


def normalize_rows(values):
    return values * lax.rsqrt(jnp.mean(values * values, axis=-1, keepdims=True) + epsilon)


def half_ex(n_ex):
    me = lax.axis_index("half") * n_ex + lax.axis_index("ex")
    return me, lambda g: {"half": g // n_ex, "ex": lax.rem(g, n_ex)}


def y_ex(n_ex):
    fr = lax.axis_index("fr")
    y = lax.rem(fr, NY)
    me = y * n_ex + lax.axis_index("ex")
    return me, lambda g: {"fr": fr - y + g // n_ex, "ex": lax.rem(g, n_ex)}


def y_only(n_ex):
    fr = lax.axis_index("fr")
    y = lax.rem(fr, NY)
    return y, lambda g: {"fr": fr - y + g}


def exchange_kernel(group, n_ex, n, stride, pick, x_ref, o_ref, ssem, rsem, lsem):
    me, device = group(n_ex)

    def peer(i):
        return lax.rem(me + i * stride, n)

    barrier = pltpu.get_barrier_semaphore()

    def greet(i, _):
        pl.semaphore_signal(barrier, inc=1, device_id=device(peer(i)), device_id_type=MESH)
        return 0

    lax.fori_loop(1, n, greet, 0)
    own = pltpu.make_async_copy(pick(x_ref, me), o_ref.at[me], lsem)
    own.start()
    pl.semaphore_wait(barrier, n - 1)

    def send(i, _):
        g = peer(i)
        pltpu.make_async_remote_copy(
            pick(x_ref, g), o_ref.at[me], ssem, rsem, device_id=device(g), device_id_type=MESH
        ).start()
        return 0

    lax.fori_loop(1, n, send, 0)
    own.wait()
    rest = o_ref.at[pl.ds(0, n - 1)]
    pltpu.make_async_copy(rest, rest, rsem).wait()
    pltpu.make_async_copy(rest, rest, ssem).wait()


def exchange(x, out_shape, group, n_ex, n, stride, pick, number):
    return pl.pallas_call(
        functools.partial(exchange_kernel, group, n_ex, n, stride, pick),
        out_shape=jax.ShapeDtypeStruct(out_shape, x.dtype),
        in_specs=[pl.BlockSpec(memory_space=pltpu.VMEM)],
        out_specs=pl.BlockSpec(memory_space=pltpu.VMEM),
        scratch_shapes=[pltpu.SemaphoreType.DMA] * 3,
        compiler_params=pltpu.CompilerParams(collective_id=number, has_side_effects=True),
        name=f"exchange_{number}",
    )(x)


def first_lanes(shape):
    lane = lax.broadcasted_iota(jnp.int32, shape, len(shape) - 1)
    return lax.rem(lane, 2 * HEAD_SIZE) < HEAD_SIZE


def normalize_heads(values, low):
    square = values * values
    low_sum = jnp.sum(jnp.where(low, square, 0.0), axis=-1, keepdims=True)
    high_sum = jnp.sum(jnp.where(low, 0.0, square), axis=-1, keepdims=True)
    scale = jnp.where(
        low,
        lax.rsqrt(low_sum * (1.0 / HEAD_SIZE) + epsilon),
        lax.rsqrt(high_sum * (1.0 / HEAD_SIZE) + epsilon),
    )
    return (values * scale).astype(jnp.bfloat16)


def project_kernel(x_ref, w_ref, q_ref, near_ref, far_ref):
    rows = x_ref.shape[1]
    pair = 2 * HEAD_SIZE
    low = first_lanes((rows, pair))
    half = rows // 2
    for c in range(3 * WIDTH // pair):
        part = jnp.dot(
            x_ref[0], w_ref[:, c * pair : (c + 1) * pair], preferred_element_type=jnp.float32
        )
        if c < 2 * WIDTH // pair:
            part = normalize_heads(part, low)
        else:
            part = part.astype(jnp.bfloat16)
        if c < WIDTH // pair:
            q_ref[0, :, c * pair : (c + 1) * pair] = part
        else:
            at = c * pair - WIDTH
            near_ref[0, :, at : at + pair] = part[:half]
            far_ref[0, :, at : at + pair] = part[half:]


def project(rows, weight):
    patches, frames, width = rows.shape
    half = frames // 2
    kv = jax.ShapeDtypeStruct((patches, half, 2 * WIDTH), jnp.bfloat16)
    return pl.pallas_call(
        project_kernel,
        grid=(patches,),
        out_shape=(jax.ShapeDtypeStruct((patches, frames, WIDTH), jnp.bfloat16), kv, kv),
        in_specs=[
            pl.BlockSpec((1, frames, width), lambda p: (p, 0, 0)),
            pl.BlockSpec(weight.shape, lambda p: (0, 0)),
        ],
        out_specs=(
            pl.BlockSpec((1, frames, WIDTH), lambda p: (p, 0, 0)),
            pl.BlockSpec((1, half, 2 * WIDTH), lambda p: (p, 0, 0)),
            pl.BlockSpec((1, half, 2 * WIDTH), lambda p: (p, 0, 0)),
        ),
        cost_estimate=pl.CostEstimate(
            flops=2 * patches * frames * width * 3 * WIDTH, bytes_accessed=6 << 20, transcendentals=0
        ),
        name="project",
    )(rows, weight)


def attend_kernel(scale_ref, start_ref, q_ref, before_ref, own_ref, o_ref):
    rows = q_ref.shape[1]
    pair = 2 * HEAD_SIZE
    low = first_lanes((rows, pair))
    query = lax.broadcasted_iota(jnp.int32, (rows, rows), 0)
    key = lax.broadcasted_iota(jnp.int32, (rows, rows), 1)
    start = start_ref[...]
    own_allowed = (key <= query) & (key >= start)
    before_allowed = (key > query) & (key - WINDOW >= start)
    contract = (((1,), (1,)), ((), ()))
    for c in range(WIDTH // pair):
        lanes = slice(c * pair, (c + 1) * pair)
        values = slice(WIDTH + c * pair, WIDTH + (c + 1) * pair)
        q = q_ref[0, :, lanes]
        outs = []
        for side in range(2):
            picked = jnp.where(low if side == 0 else ~low, q, jnp.zeros_like(q))
            factor = scale_ref[2 * c + side]
            total = None
            out = None
            for kv_ref, allowed in ((before_ref, before_allowed), (own_ref, own_allowed)):
                score = lax.dot_general(
                    picked, kv_ref[0, :, lanes], contract, preferred_element_type=jnp.float32
                )
                weight = jnp.where(allowed, jnp.exp(score * factor), 0.0)
                part_total = jnp.sum(weight, axis=-1, keepdims=True)
                part = jnp.dot(
                    weight.astype(jnp.bfloat16),
                    kv_ref[0, :, values],
                    preferred_element_type=jnp.float32,
                )
                total = part_total if total is None else total + part_total
                out = part if out is None else out + part
            outs.append(out / total)
        o_ref[0, :, lanes] = jnp.where(low, outs[0], outs[1]).astype(o_ref.dtype)


def attend(scale, start, queries, block, before, own):
    patches = queries.shape[0]
    kv_spec = pl.BlockSpec((1, WINDOW, 2 * WIDTH), lambda p: (p, 0, 0))
    return pl.pallas_call(
        attend_kernel,
        grid=(patches,),
        out_shape=jax.ShapeDtypeStruct((patches, WINDOW, WIDTH), jnp.bfloat16),
        in_specs=[
            pl.BlockSpec(memory_space=pltpu.SMEM),
            pl.BlockSpec((WINDOW, 1), lambda p: (0, 0)),
            pl.BlockSpec((1, WINDOW, WIDTH), lambda p: (p, block, 0)),
            kv_spec,
            kv_spec,
        ],
        out_specs=pl.BlockSpec((1, WINDOW, WIDTH), lambda p: (p, 0, 0)),
        cost_estimate=pl.CostEstimate(
            flops=patches * 8 * WINDOW * WINDOW * 8 * WINDOW,
            bytes_accessed=3 << 20,
            transcendentals=patches * HEADS * 2 * WINDOW * WINDOW,
        ),
        name=f"attend_{block}",
    )(scale, start, queries, before, own)


def local(
    frame_patch_tokens,
    episode_first_frame,
    router,
    expert_up_weight,
    expert_down_weight,
    query_key_value_weight,
    head_score_scale,
):
    tokens = frame_patch_tokens[0, 0]
    frame_count, patch_count, model_width = tokens.shape
    n_ex = lax.axis_size("ex")
    n_half = lax.axis_size("half")
    n_fr = lax.axis_size("fr")
    window_slots = SPE * n_ex
    tokens_wide = tokens.astype(jnp.float32)
    scaled = normalize_rows(tokens_wide).astype(jnp.bfloat16)
    logits = jnp.einsum("fpd,ds->fps", scaled, router, preferred_element_type=jnp.float32)
    dispatch = jax.nn.softmax(logits[:, :, :window_slots], axis=1).astype(jnp.bfloat16)
    slot_data = jnp.einsum(
        "fps,fpd->fsd", dispatch, tokens, preferred_element_type=jnp.float32
    ).astype(jnp.bfloat16)
    combine = jax.nn.softmax(logits, axis=2)[:, :, :window_slots]
    chunk = (frame_count * SPE, model_width)
    outgoing = slot_data.reshape(frame_count, n_ex, SPE, model_width).transpose(1, 0, 2, 3)
    outgoing = outgoing.reshape((n_ex,) + chunk)
    n = n_half * n_ex
    received = exchange(
        outgoing, (n,) + chunk, half_ex, n_ex, n, 13, lambda ref, g: ref.at[lax.rem(g, n_ex)], 0
    )
    hidden = jax.nn.gelu(
        jnp.dot(
            received.reshape(-1, model_width), expert_up_weight[0], preferred_element_type=jnp.float32
        )
    ).astype(jnp.bfloat16)
    partial_value = jnp.dot(hidden, expert_down_weight[0], preferred_element_type=jnp.float32)
    partial_value = partial_value.astype(jnp.bfloat16).reshape((n,) + chunk)
    returned = exchange(
        partial_value, (n,) + chunk, half_ex, n_ex, n, 13, lambda ref, g: ref.at[g], 1
    )
    results = returned.reshape(n_half, n_ex, frame_count, SPE, model_width).astype(jnp.float32)
    results = results.sum(axis=0)
    expert_result = results.transpose(1, 0, 2, 3).reshape(frame_count, window_slots, model_width)
    mixture = jnp.einsum("fps,fsd->fpd", combine, expert_result, precision=lax.Precision.HIGHEST)
    normed = normalize_rows(tokens_wide + mixture).astype(jnp.bfloat16)

    owners = NY * n_ex
    per = patch_count // owners
    span = n_ex * frame_count
    normed = normed.reshape(frame_count, n_ex, NY, per, model_width).transpose(2, 1, 0, 3, 4)
    normed = normed.reshape(owners, frame_count * per, model_width)
    rows = exchange(normed, normed.shape, y_ex, n_ex, owners, 37, lambda ref, g: ref.at[g], 2)
    rows = rows.reshape(NY * span, per, model_width).transpose(1, 0, 2)
    queries, near, far = project(rows, query_key_value_weight)
    route = [(i, i + NY) for i in range(n_fr - NY)]
    halo = lax.ppermute(far, "fr", route)
    base = (lax.axis_index("fr") // NY) * (NY * span)
    starts = lax.dynamic_slice_in_dim(episode_first_frame[0], base, NY * span) - base
    starts = starts[:, None]
    scale = head_score_scale / math.sqrt(HEAD_SIZE)
    late = attend(scale, starts[WINDOW:] - WINDOW, queries, 1, near, far)
    early = attend(scale, starts[:WINDOW], queries, 0, halo, near)
    attended = jnp.concatenate([early, late], axis=1).reshape(per, NY, span, WIDTH)
    back = exchange(
        attended, (NY, per, span, WIDTH), y_only, n_ex, NY, 1, lambda ref, g: ref.at[:, g], 3
    )
    return back.transpose(2, 0, 1, 3).reshape(1, span, NY * per, WIDTH)


def solution(mesh):
    placed = (
        P("half", "fr", "ex", None, None),
        P("half", None),
        P(),
        P("ex", None, "half"),
        P("ex", "half", None),
        P(),
        P(),
    )
    return jax.shard_map(
        local, mesh=mesh, in_specs=placed, out_specs=P("half", "fr", "ex", None), check_vma=False
    )
```

profile of v0, /device:TPU:10, one launch (start us, length us, event | category | flops | bytes accessed | tf_op | source)
XLA Modules:
  0.0 173.2 jit_solution(7524701388986352610)
XLA Ops:
  0.0 1.7 fusion.1
  1.7 1.9 %fusion.52 = (f32[2,256]{1,0:T(2,128)S(1)}, f32[2,256,256]{1,2,0:T(8,128)S(1)}) fusion(bf16[1024,256]{1,0:T(8,128)(2,1)} %param.9, bf16[1,1,2,256,1024]{4,3,2,1,0:T(8,128)(2,1)} %param.7, f32[2,256]{1,0:T(2,128)S(1)} %add_rsqrt_fusion.1), kind=kOutput, calls=%fused_computation.60 | convolution fusion | flops 270138880 | bytes 2101248 | tf_op jit(solution)/shard_map/fpd,ds->fps/dot_general | solution.py:227
  6.6 31.5 %exchange_0.1 = bf16[32,4,1024]{2,1,0:T(4,128)(2,1)} custom-call(bf16[16,4,1024]{2,1,0:T(4,128)(2,1)} %reshape.66.x_ref), custom_call_target="tpu_custom_call" | custom-call | tf_op jit(solution)/shard_map/exchange_0/pallas_call | solution.py:76
  39.1 3.1 %fusion.7 = bf16[128,1024]{1,0:T(8,128)(2,1)} fusion(bf16[1,1024,1024]{2,1,0:T(8,128)(2,1)S(1)} %copy-done, bf16[128,1024]{1,0:T(8,128)(2,1)S(1)} %reshape.67, bf16[1,1024,1024]{2,1,0:T(8,128)(2,1)} %param.10), kind=kOutput, calls=%fused_computation.12 | convolution fusion | flops 538181632 | bytes 4718592 | tf_op jit(solution)/shard_map/dot_general | solution.py:245
  42.3 1.7 %reshape.68.x_ref = bf16[32,4,1024]{2,1,0:T(4,128)(2,1)} reshape(bf16[128,1024]{1,0:T(8,128)(2,1)} %fusion.7) | data formatting | bytes 524288 | tf_op jit(solution)/shard_map/reshape | solution.py:246
  44.0 19.3 %exchange_1.1 = bf16[32,4,1024]{2,1,0:T(4,128)(2,1)} custom-call(bf16[32,4,1024]{2,1,0:T(4,128)(2,1)} %reshape.68.x_ref), custom_call_target="tpu_custom_call" | custom-call | tf_op jit(solution)/shard_map/exchange_1/pallas_call | solution.py:76
  63.3 2.0 %reshape.75 = f32[2,16,2,2,1024]{4,3,2,1,0:T(2,128)} reshape(bf16[32,4,1024]{2,1,0:T(4,128)(2,1)} %exchange_1.1) | data formatting | bytes 786432 | tf_op jit(solution)/shard_map/convert_element_type | solution.py:250
  65.3 1.5 reduce_sum.48
  68.0 2.1 %multiply_reduce_fusion = (f32[2,256]{1,0:T(2,128)S(1)}, f32[2,256,1024]{2,1,0:T(8,128)S(1)}) fusion(f32[2,32,1024]{2,0,1:T(2,128)S(1)} %bitcast.55, f32[2,256,256]{1,2,0:T(8,128)S(1)} %get-tuple-element.12, f32[2,256]{1,0:T(2,128)S(1)} %get-tuple-element.11, bf16[1,1,2,256,1024]{4,3,2,1,0:T(8,128)(2,1)S(1)} %copy-done.1), kind=kOutput, calls=%fused_computation.11 | convolution fusion | flops 203439616 | bytes 3477504 | tf_op jit(solution)/shard_map/fps,fsd->fpd/dot_general | solution.py:253
  70.2 1.2 multiply_convert_fusion
  71.3 1.5 reshape.70
  72.8 1.9 %copy.47 = bf16[2,16,8,2,1024]{4,3,0,1,2:T(2,128)(2,1)} copy(bf16[2,16,8,2,1024]{4,3,2,1,0:T(2,128)(2,1)S(1)} %reshape.70) | data formatting | bytes 2097152 | tf_op jit(solution)/shard_map/reshape | solution.py:259
  74.7 3.7 %reshape.71.x_ref = bf16[128,4,1024]{2,1,0:T(4,128)(2,1)} reshape(bf16[8,16,2,2,1024]{4,3,2,1,0:T(2,128)(2,1)} %bitcast.50) | data formatting | bytes 2097152 | tf_op jit(solution)/shard_map/reshape | solution.py:260
  78.4 40.6 %exchange_2.1 = bf16[128,4,1024]{2,1,0:T(4,128)(2,1)} custom-call(bf16[128,4,1024]{2,1,0:T(4,128)(2,1)} %reshape.71.x_ref), custom_call_target="tpu_custom_call" | custom-call | tf_op jit(solution)/shard_map/exchange_2/pallas_call | solution.py:76
  118.9 2.5 %reshape.72 = bf16[256,2,1024]{2,1,0:T(2,128)(2,1)S(1)} reshape(bf16[128,4,1024]{2,1,0:T(4,128)(2,1)} %exchange_2.1) | data formatting | bytes 2097152 | tf_op jit(solution)/shard_map/reshape | solution.py:262
  121.5 1.3 copy.46
  122.8 6.5 %project.1 = (bf16[2,256,512]{2,1,0:T(8,128)(2,1)}, bf16[2,128,1024]{2,1,0:T(8,128)(2,1)}, bf16[2,128,1024]{2,1,0:T(8,128)(2,1)}) custom-call(bf16[2,256,1024]{2,1,0:T(8,128)(2,1)} %bitcast.53, bf16[1024,1536]{1,0:T(8,128)(2,1)} %w_ref.1), custom_call_target="tpu_custom_call" | custom-call | flops 1610612736 | bytes 6291456 | tf_op jit(solution)/shard_map/project/pallas_call | solution.py:129
  129.3 2.9 %collective-permute-start = (bf16[2,128,1024]{2,1,0:T(8,128)(2,1)}, bf16[2,128,1024]{2,1,0:T(8,128)(2,1)S(1)}, u32[]{:S(2)}, u32[]{:S(2)}) collective-permute-start(bf16[2,128,1024]{2,1,0:T(8,128)(2,1)} %get-tuple-element.9.own_ref), channel_id=1, source_target_pairs={{0,8},{1,9},{2,10},{3,11},{4,12},{5,13},{6,14},{7,15},{8,16},{9,17... | collective-permute-start | bytes 1572872 | tf_op jit(solution)/shard_map/ppermute | solution.py:265
  134.9 5.0 %attend_1.1 = bf16[2,128,512]{2,1,0:T(8,128)(2,1)} custom-call(f32[8]{0:T(128)} %broadcast_multiply_fusion.scale_ref, s32[128,1]{1,0:T(8,128)} %copy.35.start_ref, bf16[2,256,512]{2,1,0:T(8,128)(2,1)} %get-tuple-element.8.q_ref, bf16[2,128,1024]{2,1,0:T(8,128)(2,1)} %get-tuple-element.10.own_ref.before_ref, bf16[2,128,1024]{2,1,0:T(8,128)(2,1)} %get-tuple-element.9.own_ref), custom_call_target="tpu_custom_call" | custom-call | flops 268435456 | bytes 3145728 | tf_op jit(solution)/shard_map/attend_1/pallas_call | solution.py:189
  140.0 5.2 %collective-permute-done.before_ref = bf16[2,128,1024]{2,1,0:T(8,128)(2,1)S(1)} collective-permute-done((bf16[2,128,1024]{2,1,0:T(8,128)(2,1)}, bf16[2,128,1024]{2,1,0:T(8,128)(2,1)S(1)}, u32[]{:S(2)}, u32[]{:S(2)}) %collective-permute-start) | collective-permute-done | bytes 524320 | tf_op jit(solution)/shard_map/ppermute | solution.py:265
  145.9 5.0 %attend_0.1 = bf16[2,128,512]{2,1,0:T(8,128)(2,1)} custom-call(f32[8]{0:T(128)} %broadcast_multiply_fusion.scale_ref, s32[128,1]{1,0:T(8,128)} %copy.34.start_ref, bf16[2,256,512]{2,1,0:T(8,128)(2,1)} %get-tuple-element.8.q_ref, bf16[2,128,1024]{2,1,0:T(8,128)(2,1)} %copy-done.3, bf16[2,128,1024]{2,1,0:T(8,128)(2,1)} %get-tuple-element.10.own_ref.before_ref), custom_call_target="tpu_custom_call" | custom-call | flops 268435456 | bytes 3145728 | tf_op jit(solution)/shard_map/attend_0/pallas_call | solution.py:189
  151.0 1.9 %pad_maximum_fusion = bf16[2,256,512]{2,1,0:T(8,128)(2,1)} fusion(bf16[2,128,512]{2,1,0:T(8,128)(2,1)} %attend_1.1, bf16[2,128,512]{2,1,0:T(8,128)(2,1)} %attend_0.1), kind=kLoop, calls=%fused_computation.31 | loop fusion | flops 1048576 | bytes 1048576 | tf_op jit(solution)/shard_map/concatenate | solution.py:272
  152.8 18.2 %exchange_3.1 = bf16[8,2,32,512]{3,2,1,0:T(8,128)(2,1)} custom-call(bf16[2,8,32,512]{3,2,1,0:T(8,128)(2,1)} %bitcast.51), custom_call_target="tpu_custom_call" | custom-call | tf_op jit(solution)/shard_map/exchange_3/pallas_call | solution.py:76
  171.1 2.1 %copy.36 = bf16[1,32,16,512]{3,2,1,0:T(8,128)(2,1)} copy(bf16[1,32,16,512]{3,1,2,0:T(8,128)(2,1)} %bitcast.52) | data formatting | bytes 1048576 | tf_op jit(solution)/shard_map/reshape | solution.py:276
  (25 shorter events, 8.8 us)
Async XLA Ops:
  0.0 39.1 %copy-start = (bf16[1,1024,1024]{2,1,0:T(8,128)(2,1)S(1)}, bf16[1,1024,1024]{2,1,0:T(8,128)(2,1)}, u32[]{:S(2)}) copy-start(bf16[1,1024,1024]{2,1,0:T(8,128)(2,1)} %param.11) | copy-start | bytes 6291460
  0.0 4.6 %copy-start.1 = (bf16[1,1,2,256,1024]{4,3,2,1,0:T(8,128)(2,1)S(1)}, bf16[1,1,2,256,1024]{4,3,2,1,0:T(8,128)(2,1)}, u32[]{:S(2)}) copy-start(bf16[1,1,2,256,1024]{4,3,2,1,0:T(8,128)(2,1)} %param.7) | copy-start | bytes 3145732
  3.6 0.8 copy-start.2
  122.8 11.6 %copy-start.4 = (f32[8]{0:T(128)S(1)}, f32[8]{0:T(128)}, u32[]{:S(2)}) copy-start(f32[8]{0:T(128)} %param.13) | copy-start | bytes 100
  129.3 15.8 %collective-permute-start = (bf16[2,128,1024]{2,1,0:T(8,128)(2,1)}, bf16[2,128,1024]{2,1,0:T(8,128)(2,1)S(1)}, u32[]{:S(2)}, u32[]{:S(2)}) collective-permute-start(bf16[2,128,1024]{2,1,0:T(8,128)(2,1)} %get-tuple-element.9.own_ref), channel_id=1, source_target_pairs={{0,8},{1,9},{2,10},{3,11},{4,12},{5,13},{6,14},{7,15},{8,16},{9,17... | collective-permute-start | bytes 1572872 | tf_op jit(solution)/shard_map/ppermute | solution.py:265
  145.1 0.8 copy-start.3
where the time goes:
time: 174 us; the launch traced here: 173 us
  Pallas kernels  126 us (72%)
  local copies, waits for them, and re-layouts  21.8 us (13%)
  other arithmetic  8.74 us (5%)
  matrix products  8.35 us (5%)
  waiting for transfers between devices  5.17 us (3%)
  starting transfers between devices  2.9 us (2%)
    pallas_call x4, Pallas kernels, exchange(): pl.pallas_call(functools.partial(exchange_kernel, group, n_ex, n, stride,...  110 us
    pallas_call x2, Pallas kernels, attend(): pl.pallas_call(attend_kernel, grid=(patches,), out_shape=jax.ShapeDtypeSt...  10 us
    pallas_call x1, Pallas kernels, project(): pl.pallas_call(project_kernel, grid=(patches,), out_shape=(jax.ShapeDtype...  6.52 us
    ppermute x1, waiting for transfers between devices, local(): halo = lax.ppermute(far, 'fr', route)  5.17 us
    reshape x2, local copies, waits for them, and re-layouts, local(): rows = rows.reshape(NY * span, per, model_width).transpose(1, 0, 2)  3.82 us
    reshape x1, local copies, waits for them, and re-layouts, local(): normed = normed.reshape(owners, frame_count * per, model_width)  3.68 us
  transfers between devices with their start and end apart: 1, of which 1 were waited for; matrix products, arithmetic and copies ran while one was open for 2% of the time, Pallas kernels for 3%

commit v1 on v0

v1 whole, which is shorter than its diff:
```python
import functools
import math

import jax
import jax.numpy as jnp
from jax import lax
from jax.experimental import pallas as pl
from jax.experimental.pallas import tpu as pltpu
from jax.sharding import PartitionSpec as P

SPE = 2
HEAD_SIZE = 64
HEADS = 8
WIDTH = HEADS * HEAD_SIZE
NY = 8
WINDOW = 128
MESH = pl.DeviceIdType.MESH

epsilon = 1e-06


def normalize_rows(values):
    return values * lax.rsqrt(jnp.mean(values * values, axis=-1, keepdims=True) + epsilon)


def half_ex(n_ex):
    me = lax.axis_index("half") * n_ex + lax.axis_index("ex")
    return me, lambda g: {"half": g // n_ex, "ex": lax.rem(g, n_ex)}


def y_ex(n_ex):
    fr = lax.axis_index("fr")
    y = lax.rem(fr, NY)
    me = y * n_ex + lax.axis_index("ex")
    return me, lambda g: {"fr": fr - y + g // n_ex, "ex": lax.rem(g, n_ex)}


def exchange_kernel(group, n_ex, n, stride, pick, x_ref, o_ref, ssem, rsem, lsem):
    me, device = group(n_ex)

    def peer(i):
        return lax.rem(me + i * stride, n)

    barrier = pltpu.get_barrier_semaphore()

    def greet(i, _):
        pl.semaphore_signal(barrier, inc=1, device_id=device(peer(i)), device_id_type=MESH)
        return 0

    lax.fori_loop(1, n, greet, 0)
    own = pltpu.make_async_copy(pick(x_ref, me), o_ref.at[me], lsem)
    own.start()
    pl.semaphore_wait(barrier, n - 1)

    def send(i, _):
        g = peer(i)
        pltpu.make_async_remote_copy(
            pick(x_ref, g), o_ref.at[me], ssem, rsem, device_id=device(g), device_id_type=MESH
        ).start()
        return 0

    lax.fori_loop(1, n, send, 0)
    own.wait()
    rest = o_ref.at[pl.ds(0, n - 1)]
    pltpu.make_async_copy(rest, rest, rsem).wait()
    pltpu.make_async_copy(rest, rest, ssem).wait()


def exchange(x, out_shape, group, n_ex, n, stride, pick, number):
    return pl.pallas_call(
        functools.partial(exchange_kernel, group, n_ex, n, stride, pick),
        out_shape=jax.ShapeDtypeStruct(out_shape, x.dtype),
        in_specs=[pl.BlockSpec(memory_space=pltpu.VMEM)],
        out_specs=pl.BlockSpec(memory_space=pltpu.VMEM),
        scratch_shapes=[pltpu.SemaphoreType.DMA] * 3,
        compiler_params=pltpu.CompilerParams(collective_id=number, has_side_effects=True),
        name=f"exchange_{number}",
    )(x)


def first_lanes(shape):
    lane = lax.broadcasted_iota(jnp.int32, shape, len(shape) - 1)
    return lax.rem(lane, 2 * HEAD_SIZE) < HEAD_SIZE


def normalize_heads(values, low):
    square = values * values
    low_sum = jnp.sum(jnp.where(low, square, 0.0), axis=-1, keepdims=True)
    high_sum = jnp.sum(jnp.where(low, 0.0, square), axis=-1, keepdims=True)
    scale = jnp.where(
        low,
        lax.rsqrt(low_sum * (1.0 / HEAD_SIZE) + epsilon),
        lax.rsqrt(high_sum * (1.0 / HEAD_SIZE) + epsilon),
    )
    return (values * scale).astype(jnp.bfloat16)


def attend_block(scale_ref, allowed, low, q, before, own, p, out_ref, y0):
    pair = 2 * HEAD_SIZE
    contract = (((1,), (1,)), ((), ()))
    for c in range(WIDTH // pair):
        lanes = slice(c * pair, (c + 1) * pair)
        values = slice(WIDTH + c * pair, WIDTH + (c + 1) * pair)
        queries = q(p, lanes)
        outs, scales = [], []
        for side in range(2):
            picked = jnp.where(low if side == 0 else ~low, queries, jnp.zeros_like(queries))
            factor = scale_ref[2 * c + side]
            total = None
            out = None
            for kv, mask in zip((before, own), allowed):
                score = lax.dot_general(
                    picked, kv(p, lanes), contract, preferred_element_type=jnp.float32
                )
                weight = jnp.where(mask, jnp.exp(score * factor), 0.0)
                part_total = jnp.sum(weight, axis=-1, keepdims=True)
                part = jnp.dot(
                    weight.astype(jnp.bfloat16), kv(p, values), preferred_element_type=jnp.float32
                )
                total = part_total if total is None else total + part_total
                out = part if out is None else out + part
            outs.append(out)
            scales.append(1.0 / total)
        result = jnp.where(low, outs[0], outs[1]) * jnp.where(low, scales[0], scales[1])
        result = result.astype(out_ref.dtype)
        span = out_ref.shape[2]
        for y in range(WINDOW // span):
            out_ref[p, y0 + y, :, lanes] = result[y * span : (y + 1) * span]


def tail_kernel(
    n_ex,
    scale_ref,
    start_ref,
    x_ref,
    w_hbm,
    o_ref,
    rows_ref,
    wide_ref,
    w_ref,
    q_ref,
    kv_ref,
    halo_ref,
    att_ref,
    load_sem,
    own_sem,
    send_sem,
    recv_sem,
    halo_send,
    halo_recv,
    back_send,
    back_recv,
    back_own,
):
    fr = lax.axis_index("fr")
    fx = fr // NY
    y = lax.rem(fr, NY)
    n = NY * n_ex
    n_x = lax.axis_size("fr") // NY
    me, device = y_ex(n_ex)
    after = {"fr": lax.rem(fx + 1, n_x) * NY + y}
    ahead = {"fr": lax.rem(fx + n_x - 1, n_x) * NY + y}
    load = pltpu.make_async_copy(w_hbm, w_ref, load_sem)
    load.start()

    def peer(i):
        return lax.rem(me + i * 37, n)

    barrier = pltpu.get_barrier_semaphore()

    def greet(i, _):
        pl.semaphore_signal(barrier, inc=1, device_id=device(peer(i)), device_id_type=MESH)
        return 0

    lax.fori_loop(1, n, greet, 0)
    pl.semaphore_signal(barrier, inc=1, device_id=after, device_id_type=MESH)
    pl.semaphore_signal(barrier, inc=1, device_id=ahead, device_id_type=MESH)

    def pairs(g):
        return x_ref.at[:, lax.rem(g, n_ex) * NY + g // n_ex]

    own = pltpu.make_async_copy(pairs(me), rows_ref.at[me], own_sem)
    own.start()
    pl.semaphore_wait(barrier, n + 1)

    def send(i, _):
        g = peer(i)
        pltpu.make_async_remote_copy(
            pairs(g), rows_ref.at[me], send_sem, recv_sem, device_id=device(g), device_id_type=MESH
        ).start()
        return 0

    lax.fori_loop(1, n, send, 0)
    own.wait()
    rest = rows_ref.at[pl.ds(0, n - 1)]
    pltpu.make_async_copy(rest, rest, recv_sem).wait()
    load.wait()

    frames = n * x_ref.shape[0]
    tiles = 16
    wide_ref[...] = rows_ref[...].reshape(frames * tiles, 128).astype(jnp.float32)
    pair = 2 * HEAD_SIZE
    low = first_lanes((frames, pair))
    patches = q_ref.shape[0]
    groups = tiles // patches
    inputs = []
    for p in range(patches):
        inputs.append(
            jnp.concatenate(
                [
                    wide_ref[pl.ds(p * groups + k, frames, stride=tiles), :].astype(jnp.bfloat16)
                    for k in range(groups)
                ],
                axis=1,
            )
        )
    copies = []
    for p in range(patches):
        for c in range(2 * WIDTH // 256):
            part = jnp.dot(
                inputs[p],
                w_ref[:, WIDTH + c * 256 : WIDTH + (c + 1) * 256],
                preferred_element_type=jnp.float32,
            )
            for s in range(2):
                piece = part[:, s * pair : (s + 1) * pair]
                at = c * 256 + s * pair
                if at < WIDTH:
                    piece = normalize_heads(piece, low)
                kv_ref[p, :, at : at + pair] = piece.astype(jnp.bfloat16)
        copy = pltpu.make_async_remote_copy(
            kv_ref.at[p, pl.ds(WINDOW, WINDOW)],
            halo_ref.at[p],
            halo_send.at[p],
            halo_recv.at[p],
            device_id=after,
            device_id_type=MESH,
        )
        copy.start()
        copies.append(copy)
    for p in range(patches):
        for c in range(WIDTH // 256):
            part = jnp.dot(
                inputs[p], w_ref[:, c * 256 : (c + 1) * 256], preferred_element_type=jnp.float32
            )
            for s in range(2):
                at = c * 256 + s * pair
                q_ref[p, :, at : at + pair] = normalize_heads(part[:, s * pair : (s + 1) * pair], low)

    query = lax.broadcasted_iota(jnp.int32, (WINDOW, WINDOW), 0)
    key = lax.broadcasted_iota(jnp.int32, (WINDOW, WINDOW), 1)
    low = first_lanes((WINDOW, pair))

    def masks(start):
        return (key > query) & (key - WINDOW >= start), (key <= query) & (key >= start)

    def give_back(first, last):
        for to in range(first, last):

            @pl.when(y != to)
            def _():
                pltpu.make_async_remote_copy(
                    att_ref.at[:, to],
                    o_ref.at[y],
                    back_send,
                    back_recv,
                    device_id={"fr": fr - y + to},
                    device_id_type=MESH,
                ).start()

    late = masks(start_ref[WINDOW:] - WINDOW)
    for p in range(patches):
        attend_block(
            scale_ref,
            late,
            low,
            lambda p, l: q_ref[p, WINDOW:, l],
            lambda p, l: kv_ref[p, :WINDOW, l],
            lambda p, l: kv_ref[p, WINDOW:, l],
            p,
            att_ref,
            NY // 2,
        )
    give_back(NY // 2, NY)
    early = masks(start_ref[:WINDOW])
    for p in range(patches):
        copies[p].wait()
        attend_block(
            scale_ref,
            early,
            low,
            lambda p, l: q_ref[p, :WINDOW, l],
            lambda p, l: halo_ref[p, :, l],
            lambda p, l: kv_ref[p, :WINDOW, l],
            p,
            att_ref,
            0,
        )
    give_back(0, NY // 2)
    mine = pltpu.make_async_copy(att_ref.at[:, y], o_ref.at[y], back_own)
    mine.start()
    mine.wait()
    pltpu.make_async_copy(rest, rest, send_sem).wait()
    back = o_ref.at[pl.ds(0, NY - 1)]
    pltpu.make_async_copy(back, back, back_recv).wait()
    pltpu.make_async_copy(back, back, back_send).wait()


def tail(x, weight, scale, starts, n_ex):
    frame_count = x.shape[0]
    n = NY * n_ex
    frames = n * frame_count
    patches = x.shape[2] * x.shape[3] // weight.shape[0]
    span = frames // NY
    vmem = pl.BlockSpec(memory_space=pltpu.VMEM)
    dma = pltpu.SemaphoreType.DMA
    return pl.pallas_call(
        functools.partial(tail_kernel, n_ex),
        out_shape=jax.ShapeDtypeStruct((NY, patches, span, WIDTH), jnp.bfloat16),
        in_specs=[
            pl.BlockSpec(memory_space=pltpu.SMEM),
            vmem,
            vmem,
            pl.BlockSpec(memory_space=pl.ANY),
        ],
        out_specs=vmem,
        scratch_shapes=[
            pltpu.VMEM((n, frame_count) + x.shape[2:], jnp.bfloat16),
            pltpu.VMEM((frames * x.shape[2], x.shape[3]), jnp.float32),
            pltpu.VMEM(weight.shape, jnp.bfloat16),
            pltpu.VMEM((patches, frames, WIDTH), jnp.bfloat16),
            pltpu.VMEM((patches, frames, 2 * WIDTH), jnp.bfloat16),
            pltpu.VMEM((patches, WINDOW, 2 * WIDTH), jnp.bfloat16),
            pltpu.VMEM((patches, NY, span, WIDTH), jnp.bfloat16),
            dma,
            dma,
            dma,
            dma,
            dma((patches,)),
            dma((patches,)),
            dma,
            dma,
            dma,
        ],
        compiler_params=pltpu.CompilerParams(collective_id=2, has_side_effects=True),
        name="tail",
    )(scale, starts, x, weight)


def local(
    frame_patch_tokens,
    episode_first_frame,
    router,
    expert_up_weight,
    expert_down_weight,
    query_key_value_weight,
    head_score_scale,
):
    tokens = frame_patch_tokens[0, 0]
    frame_count, patch_count, model_width = tokens.shape
    n_ex = lax.axis_size("ex")
    n_half = lax.axis_size("half")
    n_fr = lax.axis_size("fr")
    window_slots = SPE * n_ex
    tokens_wide = tokens.astype(jnp.float32)
    scaled = normalize_rows(tokens_wide).astype(jnp.bfloat16)
    logits = jnp.einsum("fpd,ds->fps", scaled, router, preferred_element_type=jnp.float32)
    dispatch = jax.nn.softmax(logits[:, :, :window_slots], axis=1).astype(jnp.bfloat16)
    slot_data = jnp.einsum(
        "fps,fpd->fsd", dispatch, tokens, preferred_element_type=jnp.float32
    ).astype(jnp.bfloat16)
    combine = jax.nn.softmax(logits, axis=2)[:, :, :window_slots]
    chunk = (frame_count * SPE, model_width)
    outgoing = slot_data.reshape(frame_count, n_ex, SPE, model_width).transpose(1, 0, 2, 3)
    outgoing = outgoing.reshape((n_ex,) + chunk)
    n = n_half * n_ex
    received = exchange(
        outgoing, (n,) + chunk, half_ex, n_ex, n, 13, lambda ref, g: ref.at[lax.rem(g, n_ex)], 0
    )
    hidden = jax.nn.gelu(
        jnp.dot(
            received.reshape(-1, model_width), expert_up_weight[0], preferred_element_type=jnp.float32
        )
    ).astype(jnp.bfloat16)
    partial_value = jnp.dot(hidden, expert_down_weight[0], preferred_element_type=jnp.float32)
    partial_value = partial_value.astype(jnp.bfloat16).reshape((n,) + chunk)
    returned = exchange(
        partial_value, (n,) + chunk, half_ex, n_ex, n, 13, lambda ref, g: ref.at[g], 1
    )
    results = returned.reshape(n_half, n_ex, frame_count, SPE, model_width).astype(jnp.float32)
    results = results.sum(axis=0)
    expert_result = results.transpose(1, 0, 2, 3).reshape(frame_count, window_slots, model_width)
    mixture = jnp.einsum("fps,fsd->fpd", combine, expert_result, precision=lax.Precision.HIGHEST)
    normed = normalize_rows(tokens_wide + mixture).astype(jnp.bfloat16)

    span = n_ex * frame_count
    per = patch_count // (NY * n_ex)
    tiles = model_width // 128
    normed = normed.reshape(frame_count, patch_count // per, per * tiles, 128)
    base = (lax.axis_index("fr") // NY) * (NY * span)
    starts = lax.dynamic_slice_in_dim(episode_first_frame[0], base, NY * span) - base
    scale = head_score_scale / math.sqrt(HEAD_SIZE)
    back = tail(normed, query_key_value_weight, scale, starts[:, None], n_ex)
    return back.transpose(2, 0, 1, 3).reshape(1, span, NY * per, WIDTH)


def solution(mesh):
    placed = (
        P("half", "fr", "ex", None, None),
        P("half", None),
        P(),
        P("ex", None, "half"),
        P("ex", "half", None),
        P(),
        P(),
    )
    return jax.shard_map(
        local, mesh=mesh, in_specs=placed, out_specs=P("half", "fr", "ex", None), check_vma=False
    )
```

time: 174 us -> 147 us (0.84)
  the two profiles are of different devices: /device:TPU:10 before, /device:TPU:47 now
where the time goes in v1:
time: 147 us; the launch traced here: 146 us
  Pallas kernels  121 us (82%)
  local copies, waits for them, and re-layouts  10.8 us (7%)
  matrix products  8.36 us (6%)
  other arithmetic  5.81 us (4%)
    pallas_call x1, Pallas kernels, tail(): pl.pallas_call(functools.partial(tail_kernel, n_ex), out_shape=jax.ShapeD...  72.8 us
    pallas_call x2, Pallas kernels, exchange(): pl.pallas_call(functools.partial(exchange_kernel, group, n_ex, n, stride,...  48.2 us
    dot_general x1, matrix products, local(): jnp.dot(hidden, expert_down_weight[0], preferred_element_type=jnp.float32)  3.16 us

profile of v1, /device:TPU:47, one launch (start us, length us, event | category | flops | bytes accessed | tf_op | source)
XLA Modules:
  0.0 146.1 jit_solution(14803991475078790696)
XLA Ops:
  0.0 0.8 subtract_bitcast_fusion
  0.8 0.8 copy.23.start_ref
  1.6 1.5 %fusion.1 = f32[2,256]{1,0:T(2,128)S(1)} fusion(bf16[1,1,2,256,1024]{4,3,2,1,0:T(8,128)(2,1)} %param.7), kind=kLoop, calls=%fused_computation.4 | loop fusion | flops 1572352 | bytes 1050624 | tf_op jit(solution)/shard_map/reduce_sum | solution.py:23
  3.1 1.9 %fusion.51 = (f32[2,256]{1,0:T(2,128)S(1)}, f32[2,256,256]{1,2,0:T(8,128)S(1)}) fusion(bf16[1024,256]{1,0:T(8,128)(2,1)} %param.9, bf16[1,1,2,256,1024]{4,3,2,1,0:T(8,128)(2,1)} %param.7, f32[2,256]{1,0:T(2,128)S(1)} %add_rsqrt_fusion.1), kind=kOutput, calls=%fused_computation.54 | convolution fusion | flops 270138880 | bytes 2101248 | tf_op jit(solution)/shard_map/fpd,ds->fps/dot_general | solution.py:367
  5.1 0.8 copy-done.2
  5.9 0.2 fusion.50
  6.1 1.1 convolution_convert_fusion
  7.3 0.1 copy.32
  7.4 0.7 reshape.58.x_ref
  8.1 31.4 %exchange_0.1 = bf16[32,4,1024]{2,1,0:T(4,128)(2,1)} custom-call(bf16[16,4,1024]{2,1,0:T(4,128)(2,1)} %reshape.58.x_ref), custom_call_target="tpu_custom_call" | custom-call | tf_op jit(solution)/shard_map/exchange_0/pallas_call | solution.py:70
  39.5 1.0 reshape.59
  40.5 3.2 %fusion.7 = bf16[128,1024]{1,0:T(8,128)(2,1)} fusion(bf16[1,1024,1024]{2,1,0:T(8,128)(2,1)S(1)} %copy-done, bf16[128,1024]{1,0:T(8,128)(2,1)S(1)} %reshape.59, bf16[1,1024,1024]{2,1,0:T(8,128)(2,1)} %param.10), kind=kOutput, calls=%fused_computation.12 | convolution fusion | flops 538181632 | bytes 4718592 | tf_op jit(solution)/shard_map/dot_general | solution.py:385
  43.6 1.7 %reshape.60.x_ref = bf16[32,4,1024]{2,1,0:T(4,128)(2,1)} reshape(bf16[128,1024]{1,0:T(8,128)(2,1)} %fusion.7) | data formatting | bytes 524288 | tf_op jit(solution)/shard_map/reshape | solution.py:386
  45.4 16.9 %exchange_1.1 = bf16[32,4,1024]{2,1,0:T(4,128)(2,1)} custom-call(bf16[32,4,1024]{2,1,0:T(4,128)(2,1)} %reshape.60.x_ref), custom_call_target="tpu_custom_call" | custom-call | tf_op jit(solution)/shard_map/exchange_1/pallas_call | solution.py:70
  62.3 2.0 %reshape.64 = f32[2,16,2,2,1024]{4,3,2,1,0:T(2,128)} reshape(bf16[32,4,1024]{2,1,0:T(4,128)(2,1)} %exchange_1.1) | data formatting | bytes 786432 | tf_op jit(solution)/shard_map/convert_element_type | solution.py:390
  64.3 1.5 reduce_sum.48
  65.7 0.1 copy.21
  65.9 1.1 fusion.49
  67.0 2.1 %multiply_reduce_fusion = (f32[2,256]{1,0:T(2,128)S(1)}, f32[2,256,1024]{2,1,0:T(8,128)S(1)}) fusion(f32[2,32,1024]{2,0,1:T(2,128)S(1)} %bitcast.43, f32[2,256,256]{1,2,0:T(8,128)S(1)} %get-tuple-element.6, f32[2,256]{1,0:T(2,128)S(1)} %get-tuple-element.5, bf16[1,1,2,256,1024]{4,3,2,1,0:T(8,128)(2,1)S(1)} %copy-done.1), kind=kOutput, calls=%fused_computation.11 | convolution fusion | flops 203439616 | bytes 3477504 | tf_op jit(solution)/shard_map/fps,fsd->fpd/dot_general | solution.py:393
  69.1 0.2 multiply_convert_fusion
  69.3 1.3 reshape.62.x_ref
  70.6 0.5 broadcast_multiply_fusion.scale_ref
  71.1 72.8 %tail.1 = bf16[8,2,32,512]{3,2,1,0:T(8,128)(2,1)} custom-call(f32[8]{0:T(128)} %broadcast_multiply_fusion.scale_ref, s32[256,1]{1,0:T(8,128)} %copy.23.start_ref, bf16[2,128,16,128]{3,2,1,0:T(8,128)(2,1)} %reshape.62.x_ref, bf16[1024,1536]{1,0:T(8,128)(2,1)} %w_hbm.1), custom_call_target="tpu_custom_call" | custom-call | tf_op jit(solution)/shard_map/tail/pallas_call | solution.py:317
  144.0 2.1 %copy.24 = bf16[1,32,16,512]{3,2,1,0:T(8,128)(2,1)} copy(bf16[1,32,16,512]{3,1,2,0:T(8,128)(2,1)} %bitcast.41) | data formatting | bytes 1048576 | tf_op jit(solution)/shard_map/reshape | solution.py:404
  (10 shorter events, 0.1 us)
Async XLA Ops:
  0.0 40.5 %copy-start = (bf16[1,1024,1024]{2,1,0:T(8,128)(2,1)S(1)}, bf16[1,1024,1024]{2,1,0:T(8,128)(2,1)}, u32[]{:S(2)}) copy-start(bf16[1,1024,1024]{2,1,0:T(8,128)(2,1)} %param.11) | copy-start | bytes 6291460
  0.0 6.1 %copy-start.1 = (bf16[1,1,2,256,1024]{4,3,2,1,0:T(8,128)(2,1)S(1)}, bf16[1,1,2,256,1024]{4,3,2,1,0:T(8,128)(2,1)}, u32[]{:S(2)}) copy-start(bf16[1,1,2,256,1024]{4,3,2,1,0:T(8,128)(2,1)} %param.7) | copy-start | bytes 3145732
  5.1 0.8 copy-start.2
  69.1 1.5 %copy-start.3 = (f32[8]{0:T(128)S(1)}, f32[8]{0:T(128)}, u32[]{:S(2)}) copy-start(f32[8]{0:T(128)} %param.13) | copy-start | bytes 100

commit v2 on v1

v2 whole, which is shorter than its diff:
```python
import functools
import math

import jax
import jax.numpy as jnp
from jax import lax
from jax.experimental import pallas as pl
from jax.experimental.pallas import tpu as pltpu
from jax.sharding import PartitionSpec as P

SPE = 2
HEAD_SIZE = 64
HEADS = 8
WIDTH = HEADS * HEAD_SIZE
NY = 8
WINDOW = 128
LANES = 128
MESH = pl.DeviceIdType.MESH

epsilon = 1e-06


def normalize_rows(values):
    return values * lax.rsqrt(jnp.mean(values * values, axis=-1, keepdims=True) + epsilon)


def first_lanes(shape):
    lane = lax.broadcasted_iota(jnp.int32, shape, len(shape) - 1)
    return lax.rem(lane, 2 * HEAD_SIZE) < HEAD_SIZE


def normalize_heads(values, low):
    square = values * values
    low_sum = jnp.sum(jnp.where(low, square, 0.0), axis=-1, keepdims=True)
    high_sum = jnp.sum(jnp.where(low, 0.0, square), axis=-1, keepdims=True)
    scale = jnp.where(
        low,
        lax.rsqrt(low_sum * (1.0 / HEAD_SIZE) + epsilon),
        lax.rsqrt(high_sum * (1.0 / HEAD_SIZE) + epsilon),
    )
    return (values * scale).astype(jnp.bfloat16)


def attend_block(scale_ref, allowed, low, q, before, own, p, out_ref, y0):
    pair = 2 * HEAD_SIZE
    contract = (((1,), (1,)), ((), ()))
    for c in range(WIDTH // pair):
        lanes = slice(c * pair, (c + 1) * pair)
        values = slice(WIDTH + c * pair, WIDTH + (c + 1) * pair)
        queries = q(p, lanes)
        outs, scales = [], []
        for side in range(2):
            picked = jnp.where(low if side == 0 else ~low, queries, jnp.zeros_like(queries))
            factor = scale_ref[2 * c + side] * (1.0 / math.sqrt(HEAD_SIZE))
            total = None
            out = None
            for kv, mask in zip((before, own), allowed):
                score = lax.dot_general(
                    picked, kv(p, lanes), contract, preferred_element_type=jnp.float32
                )
                weight = jnp.where(mask, jnp.exp(score * factor), 0.0)
                part_total = jnp.sum(weight, axis=-1, keepdims=True)
                part = jnp.dot(
                    weight.astype(jnp.bfloat16), kv(p, values), preferred_element_type=jnp.float32
                )
                total = part_total if total is None else total + part_total
                out = part if out is None else out + part
            outs.append(out)
            scales.append(1.0 / total)
        result = jnp.where(low, outs[0], outs[1]) * jnp.where(low, scales[0], scales[1])
        result = result.astype(out_ref.dtype)
        span = out_ref.shape[2]
        for y in range(WINDOW // span):
            out_ref[p, y0 + y, :, lanes] = result[y * span : (y + 1) * span]


def split(values):
    first = values.astype(jnp.bfloat16)
    rest = values - first.astype(jnp.float32)
    second = rest.astype(jnp.bfloat16)
    third = (rest - second.astype(jnp.float32)).astype(jnp.bfloat16)
    return first, second, third


def product(left, right):
    a, b, c = split(left)
    x, y, z = split(right)
    return jnp.dot(
        jnp.concatenate([a, a, b, b, a, c], axis=1),
        jnp.concatenate([x, y, x, y, z, x], axis=0),
        preferred_element_type=jnp.float32,
    )


def put_rows(wide_ref, first, values):
    rows, width = values.shape
    groups = width // LANES
    for k in range(groups):
        wide_ref[pl.ds(first + k, rows, stride=groups), :] = values[:, k * LANES : (k + 1) * LANES]


def take_rows(wide_ref, first, rows, stride, groups):
    return [wide_ref[pl.ds(first + k, rows, stride=stride), :] for k in range(groups)]


def whole_kernel(
    n_half,
    n_ex,
    scale_ref,
    start_ref,
    tok_ref,
    router_ref,
    up_hbm,
    down_hbm,
    w_hbm,
    o_ref,
    slot_ref,
    slots_in_ref,
    part_ref,
    parts_in_ref,
    combine_ref,
    x_ref,
    rows_ref,
    wide_ref,
    up_ref,
    down_ref,
    w_ref,
    q_ref,
    kv_ref,
    halo_ref,
    att_ref,
    load_sem,
    own_sem,
    slot_sem,
    part_sem,
    token_sem,
    halo_send,
    halo_recv,
    back_sem,
):
    half = lax.axis_index("half")
    ex = lax.axis_index("ex")
    fr = lax.axis_index("fr")
    fx = fr // NY
    y = lax.rem(fr, NY)
    n = NY * n_ex
    n_x = lax.axis_size("fr") // NY
    me = y * n_ex + ex
    n_he = n_half * n_ex
    me_he = half * n_ex + ex
    after = {"fr": lax.rem(fx + 1, n_x) * NY + y}
    ahead = {"fr": lax.rem(fx + n_x - 1, n_x) * NY + y}
    frame_count, patch_count, width = tok_ref.shape
    groups = width // LANES
    tiles = x_ref.shape[2]
    patches = tiles // groups

    def device(g):
        return {"fr": fr - y + g // n_ex, "ex": lax.rem(g, n_ex)}

    def peer(i):
        return lax.rem(me + i * 37, n)

    def device_he(g):
        return {"half": g // n_ex, "ex": lax.rem(g, n_ex)}

    def peer_he(i):
        return lax.rem(me_he + i * 13, n_he)

    loads = []
    for number, (source, target) in enumerate(
        ((up_hbm.at[0], up_ref), (down_hbm.at[0], down_ref), (w_hbm, w_ref))
    ):
        load = pltpu.make_async_copy(source, target, load_sem.at[number])
        load.start()
        loads.append(load)

    barrier = pltpu.get_barrier_semaphore()

    def greet(i, _):
        pl.semaphore_signal(barrier, inc=1, device_id=device(peer(i)), device_id_type=MESH)
        return 0

    def greet_other(i, _):
        other = {"half": lax.rem(half + 1, n_half), "ex": i}
        pl.semaphore_signal(barrier, inc=1, device_id=other, device_id_type=MESH)
        return 0

    lax.fori_loop(0, n_ex, greet_other, 0)
    lax.fori_loop(1, n, greet, 0)
    pl.semaphore_signal(barrier, inc=1, device_id=after, device_id_type=MESH)
    pl.semaphore_signal(barrier, inc=1, device_id=ahead, device_id_type=MESH)

    window_slots = SPE * n_ex
    for f in range(frame_count):
        wide = tok_ref[f].astype(jnp.float32)
        logits = jnp.dot(
            normalize_rows(wide).astype(jnp.bfloat16),
            router_ref[...],
            preferred_element_type=jnp.float32,
        )
        turned = jnp.transpose(logits[:, :LANES])[:window_slots]
        dispatch = jnp.exp(turned - jnp.max(turned, axis=1, keepdims=True))
        dispatch = dispatch / jnp.sum(dispatch, axis=1, keepdims=True)
        data = jnp.dot(
            dispatch.astype(jnp.bfloat16), tok_ref[f], preferred_element_type=jnp.float32
        )
        put_rows(wide_ref, f * window_slots * groups, data)
        slot_ref[f] = (
            wide_ref[f * window_slots * groups : (f + 1) * window_slots * groups]
            .astype(jnp.bfloat16)
            .reshape(slot_ref.shape[1:])
        )
        combine_ref[f] = logits

    mine = pltpu.make_async_copy(slot_ref.at[:, ex], slots_in_ref.at[me_he], own_sem.at[0])
    mine.start()
    pl.semaphore_wait(barrier, n - 1 + n_ex + 2)

    def send_slots(i, _):
        g = peer_he(i)
        pltpu.make_async_remote_copy(
            slot_ref.at[:, lax.rem(g, n_ex)],
            slots_in_ref.at[me_he],
            slot_sem.at[0],
            slot_sem.at[1],
            device_id=device_he(g),
            device_id_type=MESH,
        ).start()
        return 0

    lax.fori_loop(1, n_he, send_slots, 0)
    for f in range(frame_count):
        logits = combine_ref[f]
        combine = jnp.exp(logits - jnp.max(logits, axis=1, keepdims=True))
        combine = combine / jnp.sum(combine, axis=1, keepdims=True)
        combine_ref[f] = combine
    mine.wait()
    rest = slots_in_ref.at[pl.ds(0, n_he - 1)]
    pltpu.make_async_copy(rest, rest, slot_sem.at[1]).wait()
    loads[0].wait()
    loads[1].wait()
    rows = n_he * frame_count * SPE
    wide_ref[: rows * groups] = slots_in_ref[...].reshape(rows * groups, LANES).astype(jnp.float32)
    slot_rows = jnp.concatenate(take_rows(wide_ref, 0, rows, groups, groups), axis=1)
    hidden = jax.nn.gelu(
        jnp.dot(slot_rows.astype(jnp.bfloat16), up_ref[...], preferred_element_type=jnp.float32)
    ).astype(jnp.bfloat16)
    partial_value = jnp.dot(hidden, down_ref[...], preferred_element_type=jnp.float32)
    put_rows(wide_ref, 0, partial_value)
    part_ref[...] = wide_ref[: rows * groups].astype(jnp.bfloat16).reshape(part_ref.shape)
    mine = pltpu.make_async_copy(part_ref.at[me_he], parts_in_ref.at[me_he], own_sem.at[1])
    mine.start()

    def send_parts(i, _):
        g = peer_he(i)
        pltpu.make_async_remote_copy(
            part_ref.at[g],
            parts_in_ref.at[me_he],
            part_sem.at[0],
            part_sem.at[1],
            device_id=device_he(g),
            device_id_type=MESH,
        ).start()
        return 0

    lax.fori_loop(1, n_he, send_parts, 0)
    mine.wait()
    pltpu.make_async_copy(rest, rest, part_sem.at[1]).wait()

    pairs = patch_count // patches
    for f in range(frame_count):
        result = parts_in_ref[:n_ex, f].astype(jnp.float32)
        for h in range(1, n_half):
            result = result + parts_in_ref[h * n_ex : (h + 1) * n_ex, f].astype(jnp.float32)
        wide_ref[: window_slots * groups] = result.reshape(window_slots * groups, LANES)
        result = jnp.concatenate(take_rows(wide_ref, 0, window_slots, groups, groups), axis=1)
        mixture = product(combine_ref[f][:, :window_slots], result)
        normed = normalize_rows(tok_ref[f].astype(jnp.float32) + mixture)
        put_rows(wide_ref, 0, normed)
        x_ref[f] = (
            wide_ref[: patch_count * groups].astype(jnp.bfloat16).reshape(pairs, tiles, LANES)
        )
        mine = pltpu.make_async_copy(
            x_ref.at[f, ex * NY + y], rows_ref.at[me, f], own_sem.at[2 + f]
        )
        mine.start()

        def send_tokens(i, _):
            g = peer(i)
            pltpu.make_async_remote_copy(
                x_ref.at[f, lax.rem(g, n_ex) * NY + g // n_ex],
                rows_ref.at[me, f],
                token_sem.at[0],
                token_sem.at[1],
                device_id=device(g),
                device_id_type=MESH,
            ).start()
            return 0

        lax.fori_loop(1, n, send_tokens, 0)
        mine.wait()
    tokens_in = rows_ref.at[pl.ds(0, n - 1)]
    pltpu.make_async_copy(tokens_in, tokens_in, token_sem.at[1]).wait()
    loads[2].wait()

    frames = n * frame_count
    wide_ref[...] = rows_ref[...].reshape(frames * tiles, LANES).astype(jnp.float32)
    pair = 2 * HEAD_SIZE
    low = first_lanes((frames, pair))
    inputs = []
    for p in range(patches):
        inputs.append(
            jnp.concatenate(
                [
                    piece.astype(jnp.bfloat16)
                    for piece in take_rows(wide_ref, p * groups, frames, tiles, groups)
                ],
                axis=1,
            )
        )
    copies = []
    for p in range(patches):
        for c in range(2 * WIDTH // 256):
            part = jnp.dot(
                inputs[p],
                w_ref[:, WIDTH + c * 256 : WIDTH + (c + 1) * 256],
                preferred_element_type=jnp.float32,
            )
            for s in range(2):
                piece = part[:, s * pair : (s + 1) * pair]
                at = c * 256 + s * pair
                if at < WIDTH:
                    piece = normalize_heads(piece, low)
                kv_ref[p, :, at : at + pair] = piece.astype(jnp.bfloat16)
        copy = pltpu.make_async_remote_copy(
            kv_ref.at[p, pl.ds(WINDOW, WINDOW)],
            halo_ref.at[p],
            halo_send.at[p],
            halo_recv.at[p],
            device_id=after,
            device_id_type=MESH,
        )
        copy.start()
        copies.append(copy)
    for p in range(patches):
        for c in range(WIDTH // 256):
            part = jnp.dot(
                inputs[p], w_ref[:, c * 256 : (c + 1) * 256], preferred_element_type=jnp.float32
            )
            for s in range(2):
                at = c * 256 + s * pair
                q_ref[p, :, at : at + pair] = normalize_heads(part[:, s * pair : (s + 1) * pair], low)

    query = lax.broadcasted_iota(jnp.int32, (WINDOW, WINDOW), 0)
    key = lax.broadcasted_iota(jnp.int32, (WINDOW, WINDOW), 1)
    low = first_lanes((WINDOW, pair))

    def masks(block):
        start = start_ref[pl.ds(fx * 2 + block, 1), :] - (fx * 2 + block) * WINDOW
        start = jnp.transpose(jnp.broadcast_to(start, (WINDOW, WINDOW)))
        return (key > query) & (key - WINDOW >= start), (key <= query) & (key >= start)

    def give_back(first, last):
        for to in range(first, last):

            @pl.when(y != to)
            def _():
                pltpu.make_async_remote_copy(
                    att_ref.at[:, to],
                    o_ref.at[y],
                    back_sem.at[0],
                    back_sem.at[1],
                    device_id={"fr": fr - y + to},
                    device_id_type=MESH,
                ).start()

    late = masks(1)
    for p in range(patches):
        attend_block(
            scale_ref,
            late,
            low,
            lambda p, l: q_ref[p, WINDOW:, l],
            lambda p, l: kv_ref[p, :WINDOW, l],
            lambda p, l: kv_ref[p, WINDOW:, l],
            p,
            att_ref,
            NY // 2,
        )
    give_back(NY // 2, NY)
    early = masks(0)
    for p in range(patches):
        copies[p].wait()
        attend_block(
            scale_ref,
            early,
            low,
            lambda p, l: q_ref[p, :WINDOW, l],
            lambda p, l: halo_ref[p, :, l],
            lambda p, l: kv_ref[p, :WINDOW, l],
            p,
            att_ref,
            0,
        )
    give_back(0, NY // 2)
    mine = pltpu.make_async_copy(att_ref.at[:, y], o_ref.at[y], own_sem.at[2 + frame_count])
    mine.start()
    mine.wait()
    pltpu.make_async_copy(rest, rest, slot_sem.at[0]).wait()
    pltpu.make_async_copy(rest, rest, part_sem.at[0]).wait()
    pltpu.make_async_copy(tokens_in, tokens_in, token_sem.at[0]).wait()
    back = o_ref.at[pl.ds(0, NY - 1)]
    pltpu.make_async_copy(back, back, back_sem.at[1]).wait()
    pltpu.make_async_copy(back, back, back_sem.at[0]).wait()


def local(
    frame_patch_tokens,
    episode_first_frame,
    router,
    expert_up_weight,
    expert_down_weight,
    query_key_value_weight,
    head_score_scale,
):
    tokens = frame_patch_tokens[0, 0]
    frame_count, patch_count, width = tokens.shape
    n_ex = lax.axis_size("ex")
    n_half = lax.axis_size("half")
    n_he = n_half * n_ex
    n = NY * n_ex
    frames = n * frame_count
    span = frames // NY
    patches = patch_count // n
    groups = width // LANES
    slots = SPE * n_ex
    hidden = expert_up_weight.shape[2]
    starts = episode_first_frame.reshape(-1, WINDOW)
    vmem = pl.BlockSpec(memory_space=pltpu.VMEM)
    hbm = pl.BlockSpec(memory_space=pl.ANY)
    dma = pltpu.SemaphoreType.DMA

    def held(*shape):
        return pltpu.VMEM(shape, jnp.bfloat16)

    back = pl.pallas_call(
        functools.partial(whole_kernel, n_half, n_ex),
        out_shape=jax.ShapeDtypeStruct((NY, patches, span, WIDTH), jnp.bfloat16),
        in_specs=[pl.BlockSpec(memory_space=pltpu.SMEM), vmem, vmem, vmem, hbm, hbm, hbm],
        out_specs=vmem,
        scratch_shapes=[
            held(frame_count, n_ex, SPE * groups, LANES),
            held(n_he, frame_count, SPE * groups, LANES),
            held(n_he, frame_count, SPE * groups, LANES),
            held(n_he, frame_count, SPE * groups, LANES),
            pltpu.VMEM((frame_count, patch_count, router.shape[1]), jnp.float32),
            held(frame_count, n, patches * groups, LANES),
            held(n, frame_count, patches * groups, LANES),
            pltpu.VMEM((frames * patches * groups, LANES), jnp.float32),
            held(width, hidden),
            held(hidden, width),
            held(*query_key_value_weight.shape),
            held(patches, frames, WIDTH),
            held(patches, frames, 2 * WIDTH),
            held(patches, WINDOW, 2 * WIDTH),
            held(patches, NY, span, WIDTH),
            dma((3,)),
            dma((3 + frame_count,)),
            dma((2,)),
            dma((2,)),
            dma((2,)),
            dma((patches,)),
            dma((patches,)),
            dma((2,)),
        ],
        compiler_params=pltpu.CompilerParams(collective_id=0, has_side_effects=True),
        name="whole",
    )(
        head_score_scale,
        starts,
        tokens,
        router,
        expert_up_weight,
        expert_down_weight,
        query_key_value_weight,
    )
    return back.transpose(2, 0, 1, 3).reshape(1, span, NY * patches, WIDTH)


def solution(mesh):
    placed = (
        P("half", "fr", "ex", None, None),
        P("half", None),
        P(),
        P("ex", None, "half"),
        P("ex", "half", None),
        P(),
        P(),
    )
    return jax.shard_map(
        local, mesh=mesh, in_specs=placed, out_specs=P("half", "fr", "ex", None), check_vma=False
    )
```

time: 147 us -> 109 us (0.74)
  Pallas kernels: 121 us -> 105 us
  local copies, waits for them, and re-layouts: 10.8 us -> 2.13 us
  matrix products: 8.36 us -> 0 us
  other arithmetic: 5.81 us -> 0 us
    pallas_call x3 -> x1, Pallas kernels: 121 us -> 105 us  [local(): pl.pallas_call(functools.partial(whole_kernel, n_half, n_ex), out_shape=j...]
    dot_general x4 -> x0, matrix products: 8.36 us -> none  [the longest x1 3.16 us: local(): jnp.dot(hidden, expert_down_weight[0], preferred_element_type=jnp.float32)]
    reshape x7 -> x1, local copies, waits for them, and re-layouts: 7.06 us -> 2.13 us  [local(): return back.transpose(2, 0, 1, 3).reshape(1, span, NY * patches, WIDTH)]
    reduce_sum x3 -> x0, other arithmetic: 4.1 us -> none  [the longest x1 1.5 us: normalize_rows(): jnp.mean(values * values, axis=-1, keepdims=True) + epsilon]
    convert_element_type x1 -> x0, local copies, waits for them, and re-layouts: 1.99 us -> none  [local(): returned.reshape(n_half, n_ex, frame_count, SPE, model_width)]
where the time goes in v2:
time: 109 us; the launch traced here: 107 us
  Pallas kernels  105 us (96%)
  local copies, waits for them, and re-layouts  2.13 us (2%)
    pallas_call x1, Pallas kernels, local(): pl.pallas_call(functools.partial(whole_kernel, n_half, n_ex), out_shape=j...  105 us

profile of v2, /device:TPU:47, one launch (start us, length us, event | category | flops | bytes accessed | tf_op | source)
XLA Modules:
  0.0 107.3 jit_solution(6519400430212330303)
XLA Ops:
  0.0 105.2 %whole.1 = bf16[8,2,32,512]{3,2,1,0:T(8,128)(2,1)} custom-call(f32[8]{0:T(128)} %scale_ref.1, s32[8,128]{1,0:T(8,128)} %bitcast.7, bf16[2,256,1024]{2,1,0:T(8,128)(2,1)} %bitcast.6, bf16[1024,256]{1,0:T(8,128)(2,1)} %router_ref.1, bf16[1,1024,1024]{2,1,0:T(8,128)(2,1)} %up_hbm.1, bf16[1,1024,1024]{2,1,0:T(8,128)(2,1)} %down_hbm.1, bf16[1024,1536]{1,0:T(8,128)(2,1)} %w_hbm.1), custom_call_target="tpu_custom_call" | custom-call | tf_op jit(solution)/shard_map/whole/pallas_call | solution.py:447
  105.2 2.1 %copy.8 = bf16[1,32,16,512]{3,2,1,0:T(8,128)(2,1)} copy(bf16[1,32,16,512]{3,1,2,0:T(8,128)(2,1)} %bitcast.5) | data formatting | bytes 1048576 | tf_op jit(solution)/shard_map/reshape | solution.py:488

commit v3 on v2

--- a/solution.py
+++ b/solution.py
@@ -133,7 +133,8 @@
     own_sem,
     slot_sem,
     part_sem,
-    token_sem,
+    token_send,
+    token_recv,
     halo_send,
     halo_recv,
     back_sem,
@@ -152,8 +153,7 @@
     ahead = {"fr": lax.rem(fx + n_x - 1, n_x) * NY + y}
     frame_count, patch_count, width = tok_ref.shape
     groups = width // LANES
-    tiles = x_ref.shape[2]
-    patches = tiles // groups
+    patches = q_ref.shape[0]
 
     def device(g):
         return {"fr": fr - y + g // n_ex, "ex": lax.rem(g, n_ex)}
@@ -278,52 +278,86 @@
         mixture = product(combine_ref[f][:, :window_slots], result)
         normed = normalize_rows(tok_ref[f].astype(jnp.float32) + mixture)
         put_rows(wide_ref, 0, normed)
-        x_ref[f] = (
-            wide_ref[: patch_count * groups].astype(jnp.bfloat16).reshape(pairs, tiles, LANES)
-        )
-        mine = pltpu.make_async_copy(
-            x_ref.at[f, ex * NY + y], rows_ref.at[me, f], own_sem.at[2 + f]
-        )
-        mine.start()
+        packed = wide_ref[: patch_count * groups].reshape(pairs, patches * groups, LANES)
+        for p in range(patches):
+            x_ref[p, f] = packed[:, p * groups : (p + 1) * groups].astype(jnp.bfloat16)
 
         def send_tokens(i, _):
             g = peer(i)
             pltpu.make_async_remote_copy(
-                x_ref.at[f, lax.rem(g, n_ex) * NY + g // n_ex],
-                rows_ref.at[me, f],
-                token_sem.at[0],
-                token_sem.at[1],
+                x_ref.at[0, f, lax.rem(g, n_ex) * NY + g // n_ex],
+                rows_ref.at[0, me, f],
+                token_send.at[0],
+                token_recv.at[0],
                 device_id=device(g),
                 device_id_type=MESH,
             ).start()
             return 0
 
         lax.fori_loop(1, n, send_tokens, 0)
-        mine.wait()
-    tokens_in = rows_ref.at[pl.ds(0, n - 1)]
-    pltpu.make_async_copy(tokens_in, tokens_in, token_sem.at[1]).wait()
+    owns = []
+    for p in range(patches):
+        mine = pltpu.make_async_copy(
+            x_ref.at[p, :, ex * NY + y], rows_ref.at[p, me], own_sem.at[2 + p]
+        )
+        mine.start()
+        owns.append(mine)
+        if p == 0:
+            continue
+
+        def send_later(i, _):
+            g = peer(i)
+            pltpu.make_async_remote_copy(
+                x_ref.at[p, :, lax.rem(g, n_ex) * NY + g // n_ex],
+                rows_ref.at[p, me],
+                token_send.at[p],
+                token_recv.at[p],
+                device_id=device(g),
+                device_id_type=MESH,
+            ).start()
+            return 0
+
+        lax.fori_loop(1, n, send_later, 0)
     loads[2].wait()
 
     frames = n * frame_count
-    wide_ref[...] = rows_ref[...].reshape(frames * tiles, LANES).astype(jnp.float32)
     pair = 2 * HEAD_SIZE
-    low = first_lanes((frames, pair))
-    inputs = []
+    all_low = first_lanes((frames, pair))
+    low = first_lanes((WINDOW, pair))
+    query = lax.broadcasted_iota(jnp.int32, (WINDOW, WINDOW), 0)
+    key = lax.broadcasted_iota(jnp.int32, (WINDOW, WINDOW), 1)
+
+    def masks(block):
+        start = start_ref[pl.ds(fx * 2 + block, 1), :] - (fx * 2 + block) * WINDOW
+        start = jnp.transpose(jnp.broadcast_to(start, (WINDOW, WINDOW)))
+        return (key > query) & (key - WINDOW >= start), (key <= query) & (key >= start)
+
+    late, early = masks(1), masks(0)
+
+    def give_back(p, first, last):
+        for to in range(first, last):
+
+            @pl.when(y != to)
+            def _():
+                pltpu.make_async_remote_copy(
+                    att_ref.at[p, to],
+                    o_ref.at[y, p],
+                    back_sem.at[0],
+                    back_sem.at[1],
+                    device_id={"fr": fr - y + to},
+                    device_id_type=MESH,
+                ).start()
+
     for p in range(patches):
-        inputs.append(
-            jnp.concatenate(
-                [
-                    piece.astype(jnp.bfloat16)
-                    for piece in take_rows(wide_ref, p * groups, frames, tiles, groups)
-                ],
-                axis=1,
-            )
-        )
-    copies = []
-    for p in range(patches):
+        owns[p].wait()
+        tokens_in = rows_ref.at[p, pl.ds(0, n - 1)]
+        pltpu.make_async_copy(tokens_in, tokens_in, token_recv.at[p]).wait()
+        wide_ref[...] = rows_ref[p].reshape(frames * groups, LANES).astype(jnp.float32)
+        taken = take_rows(wide_ref, 0, frames, groups, groups)
+        inputs = jnp.concatenate([piece.astype(jnp.bfloat16) for piece in taken], axis=1)
         for c in range(2 * WIDTH // 256):
             part = jnp.dot(
-                inputs[p],
+                inputs,
                 w_ref[:, WIDTH + c * 256 : WIDTH + (c + 1) * 256],
                 preferred_element_type=jnp.float32,
             )
@@ -331,9 +365,9 @@
                 piece = part[:, s * pair : (s + 1) * pair]
                 at = c * 256 + s * pair
                 if at < WIDTH:
-                    piece = normalize_heads(piece, low)
+                    piece = normalize_heads(piece, all_low)
                 kv_ref[p, :, at : at + pair] = piece.astype(jnp.bfloat16)
-        copy = pltpu.make_async_remote_copy(
+        halo = pltpu.make_async_remote_copy(
             kv_ref.at[p, pl.ds(WINDOW, WINDOW)],
             halo_ref.at[p],
             halo_send.at[p],
@@ -341,42 +375,16 @@
             device_id=after,
             device_id_type=MESH,
         )
-        copy.start()
-        copies.append(copy)
-    for p in range(patches):
+        halo.start()
         for c in range(WIDTH // 256):
             part = jnp.dot(
-                inputs[p], w_ref[:, c * 256 : (c + 1) * 256], preferred_element_type=jnp.float32
+                inputs, w_ref[:, c * 256 : (c + 1) * 256], preferred_element_type=jnp.float32
             )
             for s in range(2):
                 at = c * 256 + s * pair
-                q_ref[p, :, at : at + pair] = normalize_heads(part[:, s * pair : (s + 1) * pair], low)
-
-    query = lax.broadcasted_iota(jnp.int32, (WINDOW, WINDOW), 0)
-    key = lax.broadcasted_iota(jnp.int32, (WINDOW, WINDOW), 1)
-    low = first_lanes((WINDOW, pair))
-
-    def masks(block):
-        start = start_ref[pl.ds(fx * 2 + block, 1), :] - (fx * 2 + block) * WINDOW
-        start = jnp.transpose(jnp.broadcast_to(start, (WINDOW, WINDOW)))
-        return (key > query) & (key - WINDOW >= start), (key <= query) & (key >= start)
-
-    def give_back(first, last):
-        for to in range(first, last):
-
-            @pl.when(y != to)
-            def _():
-                pltpu.make_async_remote_copy(
-                    att_ref.at[:, to],
-                    o_ref.at[y],
-                    back_sem.at[0],
-                    back_sem.at[1],
-                    device_id={"fr": fr - y + to},
-                    device_id_type=MESH,
-                ).start()
-
-    late = masks(1)
-    for p in range(patches):
+                q_ref[p, :, at : at + pair] = normalize_heads(
+                    part[:, s * pair : (s + 1) * pair], all_low
+                )
         attend_block(
             scale_ref,
             late,
@@ -388,10 +396,8 @@
             att_ref,
             NY // 2,
         )
-    give_back(NY // 2, NY)
-    early = masks(0)
-    for p in range(patches):
-        copies[p].wait()
+        give_back(p, NY // 2, NY)
+        halo.wait()
         attend_block(
             scale_ref,
             early,
@@ -403,13 +409,15 @@
             att_ref,
             0,
         )
-    give_back(0, NY // 2)
-    mine = pltpu.make_async_copy(att_ref.at[:, y], o_ref.at[y], own_sem.at[2 + frame_count])
+        give_back(p, 0, NY // 2)
+    mine = pltpu.make_async_copy(att_ref.at[:, y], o_ref.at[y], own_sem.at[2 + patches])
     mine.start()
     mine.wait()
     pltpu.make_async_copy(rest, rest, slot_sem.at[0]).wait()
     pltpu.make_async_copy(rest, rest, part_sem.at[0]).wait()
-    pltpu.make_async_copy(tokens_in, tokens_in, token_sem.at[0]).wait()
+    for p in range(patches):
+        tokens_in = rows_ref.at[p, pl.ds(0, n - 1)]
+        pltpu.make_async_copy(tokens_in, tokens_in, token_send.at[p]).wait()
     back = o_ref.at[pl.ds(0, NY - 1)]
     pltpu.make_async_copy(back, back, back_sem.at[1]).wait()
     pltpu.make_async_copy(back, back, back_sem.at[0]).wait()
@@ -455,9 +463,9 @@
             held(n_he, frame_count, SPE * groups, LANES),
             held(n_he, frame_count, SPE * groups, LANES),
             pltpu.VMEM((frame_count, patch_count, router.shape[1]), jnp.float32),
-            held(frame_count, n, patches * groups, LANES),
-            held(n, frame_count, patches * groups, LANES),
-            pltpu.VMEM((frames * patches * groups, LANES), jnp.float32),
+            held(patches, frame_count, n, groups, LANES),
+            held(patches, n, frame_count, groups, LANES),
+            pltpu.VMEM((frames * groups, LANES), jnp.float32),
             held(width, hidden),
             held(hidden, width),
             held(*query_key_value_weight.shape),
@@ -466,10 +474,11 @@
             held(patches, WINDOW, 2 * WIDTH),
             held(patches, NY, span, WIDTH),
             dma((3,)),
-            dma((3 + frame_count,)),
+            dma((3 + patches,)),
             dma((2,)),
             dma((2,)),
-            dma((2,)),
+            dma((patches,)),
+            dma((patches,)),
             dma((patches,)),
             dma((patches,)),
             dma((2,)),

time: 109 us -> 98.5 us (0.904)
  the two profiles are of different devices: /device:TPU:47 before, /device:TPU:44 now
where the time goes in v3:
time: 98.5 us; the launch traced here: 98.3 us
  Pallas kernels  96.2 us (98%)
  local copies, waits for them, and re-layouts  2.13 us (2%)
    pallas_call x1, Pallas kernels, local(): pl.pallas_call(functools.partial(whole_kernel, n_half, n_ex), out_shape=j...  96.2 us
    reshape x1, local copies, waits for them, and re-layouts, local(): return back.transpose(2, 0, 1, 3).reshape(1, span, NY * patches, WIDTH)  2.13 us

profile of v3, /device:TPU:44, one launch (start us, length us, event | category | flops | bytes accessed | tf_op | source)
XLA Modules:
  0.0 98.3 jit_solution(429205686020651846)
XLA Ops:
  0.0 96.2 %whole.1 = bf16[8,2,32,512]{3,2,1,0:T(8,128)(2,1)} custom-call(f32[8]{0:T(128)} %scale_ref.1, s32[8,128]{1,0:T(8,128)} %bitcast.7, bf16[2,256,1024]{2,1,0:T(8,128)(2,1)} %bitcast.6, bf16[1024,256]{1,0:T(8,128)(2,1)} %router_ref.1, bf16[1,1024,1024]{2,1,0:T(8,128)(2,1)} %up_hbm.1, bf16[1,1024,1024]{2,1,0:T(8,128)(2,1)} %down_hbm.1, bf16[1024,1536]{1,0:T(8,128)(2,1)} %w_hbm.1), custom_call_target="tpu_custom_call" | custom-call | tf_op jit(solution)/shard_map/whole/pallas_call | solution.py:455
  96.2 2.1 %copy.8 = bf16[1,32,16,512]{3,2,1,0:T(8,128)(2,1)} copy(bf16[1,32,16,512]{3,1,2,0:T(8,128)(2,1)} %bitcast.5) | data formatting | bytes 1048576 | tf_op jit(solution)/shard_map/reshape | solution.py:497

commit v4 on v3

v4 whole, which is shorter than its diff:
```python
import functools
import math

import jax
import jax.numpy as jnp
from jax import lax
from jax.experimental import pallas as pl
from jax.experimental.pallas import tpu as pltpu
from jax.sharding import PartitionSpec as P

SPE = 2
HEAD_SIZE = 64
HEADS = 8
WIDTH = HEADS * HEAD_SIZE
NY = 8
WINDOW = 128
LANES = 128
MESH = pl.DeviceIdType.MESH

epsilon = 1e-06


def normalize_rows(values):
    return values * lax.rsqrt(jnp.mean(values * values, axis=-1, keepdims=True) + epsilon)


def first_lanes(shape):
    lane = lax.broadcasted_iota(jnp.int32, shape, len(shape) - 1)
    return lax.rem(lane, 2 * HEAD_SIZE) < HEAD_SIZE


def normalize_heads(values, low):
    square = values * values
    low_sum = jnp.sum(jnp.where(low, square, 0.0), axis=-1, keepdims=True)
    high_sum = jnp.sum(jnp.where(low, 0.0, square), axis=-1, keepdims=True)
    scale = jnp.where(
        low,
        lax.rsqrt(low_sum * (1.0 / HEAD_SIZE) + epsilon),
        lax.rsqrt(high_sum * (1.0 / HEAD_SIZE) + epsilon),
    )
    return (values * scale).astype(jnp.bfloat16)


def attend_block(scale_ref, allowed, low, q, before, own, p, out_ref, y0, enter, leave):
    pair = 2 * HEAD_SIZE
    contract = (((1,), (1,)), ((), ()))
    for c in range(WIDTH // pair):
        lanes = slice(c * pair, (c + 1) * pair)
        keys = slice(2 * c * pair, (2 * c + 1) * pair)
        values = slice((2 * c + 1) * pair, (2 * c + 2) * pair)
        enter(c)
        queries = q(p, lanes)
        outs, scales = [], []
        for side in range(2):
            picked = jnp.where(low if side == 0 else ~low, queries, jnp.zeros_like(queries))
            factor = scale_ref[2 * c + side] * (1.0 / math.sqrt(HEAD_SIZE))
            total = None
            out = None
            for kv, mask in zip((before, own), allowed):
                score = lax.dot_general(
                    picked, kv(p, keys), contract, preferred_element_type=jnp.float32
                )
                weight = jnp.where(mask, jnp.exp(score * factor), 0.0)
                part_total = jnp.sum(weight, axis=-1, keepdims=True)
                part = jnp.dot(
                    weight.astype(jnp.bfloat16), kv(p, values), preferred_element_type=jnp.float32
                )
                total = part_total if total is None else total + part_total
                out = part if out is None else out + part
            outs.append(out)
            scales.append(1.0 / total)
        result = jnp.where(low, outs[0], outs[1]) * jnp.where(low, scales[0], scales[1])
        result = result.astype(out_ref.dtype)
        span = out_ref.shape[2]
        for y in range(WINDOW // span):
            out_ref[p, y0 + y, :, lanes] = result[y * span : (y + 1) * span]
        leave(c)


def split(values):
    first = values.astype(jnp.bfloat16)
    rest = values - first.astype(jnp.float32)
    second = rest.astype(jnp.bfloat16)
    third = (rest - second.astype(jnp.float32)).astype(jnp.bfloat16)
    return first, second, third


def product(left, right):
    a, b, c = split(left)
    x, y, z = split(right)
    return jnp.dot(
        jnp.concatenate([a, a, b, b, a, c], axis=1),
        jnp.concatenate([x, y, x, y, z, x], axis=0),
        preferred_element_type=jnp.float32,
    )


def put_rows(wide_ref, first, values):
    rows, width = values.shape
    groups = width // LANES
    for k in range(groups):
        wide_ref[pl.ds(first + k, rows, stride=groups), :] = values[:, k * LANES : (k + 1) * LANES]


def take_rows(wide_ref, first, rows, stride, groups):
    return [wide_ref[pl.ds(first + k, rows, stride=stride), :] for k in range(groups)]


def whole_kernel(
    n_half,
    n_ex,
    scale_ref,
    start_ref,
    tok_hbm,
    router_hbm,
    up_hbm,
    down_hbm,
    w_hbm,
    o_ref,
    tok_ref,
    router_ref,
    slot_ref,
    slots_in_ref,
    part_ref,
    parts_in_ref,
    combine_ref,
    x_ref,
    rows_ref,
    wide_ref,
    up_ref,
    down_ref,
    w_ref,
    q_ref,
    kv_ref,
    halo_ref,
    att_ref,
    load_sem,
    own_sem,
    slot_sem,
    part_sem,
    token_send,
    token_recv,
    halo_send,
    halo_recv,
    back_sem,
):
    half = lax.axis_index("half")
    ex = lax.axis_index("ex")
    fr = lax.axis_index("fr")
    fx = fr // NY
    y = lax.rem(fr, NY)
    n = NY * n_ex
    n_x = lax.axis_size("fr") // NY
    me = y * n_ex + ex
    n_he = n_half * n_ex
    me_he = half * n_ex + ex
    after = {"fr": lax.rem(fx + 1, n_x) * NY + y}
    ahead = {"fr": lax.rem(fx + n_x - 1, n_x) * NY + y}
    frame_count, patch_count, width = tok_ref.shape
    groups = width // LANES
    patches = q_ref.shape[0]

    ys = [lax.rem(y + d, NY) for d in range(NY)]
    frs = [fr - y + to for to in ys]
    other = lax.rem(half + 1, n_half)
    pair = 2 * HEAD_SIZE
    head_pairs = WIDTH // pair

    def turn(i):
        return lax.rem(ex + i * 5, n_ex)

    barrier = pltpu.get_barrier_semaphore()

    def signal(device):
        pl.semaphore_signal(barrier, inc=1, device_id=device, device_id_type=MESH)

    signal({"half": other})
    for d in range(1, NY):
        signal({"fr": frs[d]})
    signal(after)
    signal(ahead)

    def greet(i, _):
        e = turn(i)
        signal({"half": other, "ex": e})
        for d in range(NY):
            signal({"fr": frs[d], "ex": e})
        return 0

    first_loads = [
        pltpu.make_async_copy(tok_hbm.at[0, 0], tok_ref, load_sem.at[0]),
        pltpu.make_async_copy(router_hbm, router_ref, load_sem.at[1]),
    ]
    loads = [
        pltpu.make_async_copy(up_hbm.at[0], up_ref, load_sem.at[2]),
        pltpu.make_async_copy(down_hbm.at[0], down_ref, load_sem.at[3]),
    ]
    for load in first_loads:
        load.start()
    lax.fori_loop(1, n_ex, greet, 0)
    for load in loads:
        load.start()
    for c in range(head_pairs):
        for part, at in ((1, 2 * c), (2, 2 * c + 1), (0, 2 * head_pairs + c)):
            pltpu.make_async_copy(
                w_hbm.at[:, pl.ds(part * WIDTH + c * pair, pair)],
                w_ref.at[:, pl.ds(at * pair, pair)],
                load_sem.at[4],
            ).start()
    for load in first_loads:
        load.wait()

    window_slots = SPE * n_ex
    block = window_slots * groups

    def send_all(pick, place, sems, f):
        def one(h, e):
            device = {"half": h, "ex": e}
            pltpu.make_async_remote_copy(
                pick(h, e),
                place,
                sems.at[0, f],
                sems.at[1, f],
                device_id=device,
                device_id_type=MESH,
            ).start()

        def step(i, _):
            e = turn(i)
            one(other, e)
            one(half, e)
            return 0

        one(other, ex)
        lax.fori_loop(1, n_ex, step, 0)

    slot_owns = []
    for f in range(frame_count):
        wide = tok_ref[f].astype(jnp.float32)
        logits = jnp.dot(
            normalize_rows(wide).astype(jnp.bfloat16),
            router_ref[...],
            preferred_element_type=jnp.float32,
        )
        turned = jnp.transpose(logits[:, :LANES])[:window_slots]
        dispatch = jnp.exp(turned - jnp.max(turned, axis=1, keepdims=True))
        dispatch = dispatch / jnp.sum(dispatch, axis=1, keepdims=True)
        data = jnp.dot(
            dispatch.astype(jnp.bfloat16), tok_ref[f], preferred_element_type=jnp.float32
        )
        put_rows(wide_ref, f * block, data)
        slot_ref[f] = (
            wide_ref[f * block : (f + 1) * block]
            .astype(jnp.bfloat16)
            .reshape(slot_ref.shape[1:])
        )
        if f == 0:
            pl.semaphore_wait(barrier, n - 1 + n_ex + 2)
        mine = pltpu.make_async_copy(slot_ref.at[f, ex], slots_in_ref.at[f, me_he], own_sem.at[f])
        mine.start()
        slot_owns.append(mine)
        send_all(lambda h, e: slot_ref.at[f, e], slots_in_ref.at[f, me_he], slot_sem, f)
        combine = jnp.exp(logits - jnp.max(logits, axis=1, keepdims=True))
        combine_ref[f] = combine / jnp.sum(combine, axis=1, keepdims=True)

    rows = n_he * SPE
    part_owns = []
    for f in range(frame_count):
        slot_owns[f].wait()
        rest = slots_in_ref.at[f, pl.ds(0, n_he - 1)]
        pltpu.make_async_copy(rest, rest, slot_sem.at[1, f]).wait()
        if f == 0:
            loads[0].wait()
            loads[1].wait()
        wide_ref[: rows * groups] = (
            slots_in_ref[f].reshape(rows * groups, LANES).astype(jnp.float32)
        )
        slot_rows = jnp.concatenate(take_rows(wide_ref, 0, rows, groups, groups), axis=1)
        hidden = jax.nn.gelu(
            jnp.dot(slot_rows.astype(jnp.bfloat16), up_ref[...], preferred_element_type=jnp.float32)
        ).astype(jnp.bfloat16)
        partial_value = jnp.dot(hidden, down_ref[...], preferred_element_type=jnp.float32)
        put_rows(wide_ref, 0, partial_value)
        part_ref[f] = (
            wide_ref[: rows * groups].astype(jnp.bfloat16).reshape(part_ref.shape[1:])
        )
        mine = pltpu.make_async_copy(
            part_ref.at[f, me_he], parts_in_ref.at[f, me_he], own_sem.at[frame_count + f]
        )
        mine.start()
        part_owns.append(mine)
        send_all(
            lambda h, e: part_ref.at[f, h * n_ex + e], parts_in_ref.at[f, me_he], part_sem, f
        )

    pairs = patch_count // patches

    def send_group(pick, place, p):
        def one(d, e):
            pltpu.make_async_remote_copy(
                pick(e * NY + ys[d]),
                place,
                token_send.at[p],
                token_recv.at[p],
                device_id={"fr": frs[d], "ex": e},
                device_id_type=MESH,
            ).start()

        def step(i, _):
            e = turn(i)
            for d in range(NY):
                one(d, e)
            return 0

        for d in range(1, NY):
            one(d, ex)
        lax.fori_loop(1, n_ex, step, 0)

    for f in range(frame_count):
        part_owns[f].wait()
        rest = parts_in_ref.at[f, pl.ds(0, n_he - 1)]
        pltpu.make_async_copy(rest, rest, part_sem.at[1, f]).wait()
        result = parts_in_ref[f, :n_ex].astype(jnp.float32)
        for h in range(1, n_half):
            result = result + parts_in_ref[f, h * n_ex : (h + 1) * n_ex].astype(jnp.float32)
        wide_ref[: window_slots * groups] = result.reshape(window_slots * groups, LANES)
        result = jnp.concatenate(take_rows(wide_ref, 0, window_slots, groups, groups), axis=1)
        mixture = product(combine_ref[f][:, :window_slots], result)
        normed = normalize_rows(tok_ref[f].astype(jnp.float32) + mixture)
        put_rows(wide_ref, 0, normed)
        packed = wide_ref[: patch_count * groups].reshape(pairs, patches * groups, LANES)
        for p in range(patches):
            x_ref[p, f] = packed[:, p * groups : (p + 1) * groups].astype(jnp.bfloat16)

        send_group(lambda at: x_ref.at[0, f, at], rows_ref.at[0, me, f], 0)
    owns = []
    for p in range(patches):
        mine = pltpu.make_async_copy(
            x_ref.at[p, :, ex * NY + y], rows_ref.at[p, me], own_sem.at[2 * frame_count + p]
        )
        mine.start()
        owns.append(mine)
        if p == 0:
            continue

        send_group(lambda at: x_ref.at[p, :, at], rows_ref.at[p, me], p)
    pltpu.make_async_copy(w_ref, w_ref, load_sem.at[4]).wait()

    frames = n * frame_count
    all_low = first_lanes((frames, pair))
    low = first_lanes((WINDOW, pair))
    query = lax.broadcasted_iota(jnp.int32, (WINDOW, WINDOW), 0)
    key = lax.broadcasted_iota(jnp.int32, (WINDOW, WINDOW), 1)

    def masks(block):
        start = start_ref[pl.ds(fx * 2 + block, 1), :] - (fx * 2 + block) * WINDOW
        start = jnp.transpose(jnp.broadcast_to(start, (WINDOW, WINDOW)))
        return (key > query) & (key - WINDOW >= start), (key <= query) & (key >= start)

    late, early = masks(1), masks(0)

    def give_back(p, first, last, at, lanes):
        for to in range(first, last):

            @pl.when(y != to)
            def _():
                pltpu.make_async_remote_copy(
                    att_ref.at[p, to, :, pl.ds(at, lanes)],
                    o_ref.at[y, p, :, pl.ds(at, lanes)],
                    back_sem.at[0],
                    back_sem.at[1],
                    device_id={"fr": fr - y + to},
                    device_id_type=MESH,
                ).start()

    for p in range(patches):
        owns[p].wait()
        tokens_in = rows_ref.at[p, pl.ds(0, n - 1)]
        pltpu.make_async_copy(tokens_in, tokens_in, token_recv.at[p]).wait()
        wide_ref[...] = rows_ref[p].reshape(frames * groups, LANES).astype(jnp.float32)
        taken = take_rows(wide_ref, 0, frames, groups, groups)
        inputs = jnp.concatenate([piece.astype(jnp.bfloat16) for piece in taken], axis=1)
        halos = []
        for c in range(head_pairs):
            lanes = slice(2 * c * pair, (2 * c + 2) * pair)
            part = jnp.dot(inputs, w_ref[:, lanes], preferred_element_type=jnp.float32)
            kv_ref[p, :, 2 * c * pair : (2 * c + 1) * pair] = normalize_heads(
                part[:, :pair], all_low
            )
            kv_ref[p, :, (2 * c + 1) * pair : (2 * c + 2) * pair] = part[:, pair:].astype(
                jnp.bfloat16
            )
            halo = pltpu.make_async_remote_copy(
                kv_ref.at[p, pl.ds(WINDOW, WINDOW), pl.ds(2 * c * pair, 2 * pair)],
                halo_ref.at[p, :, pl.ds(2 * c * pair, 2 * pair)],
                halo_send.at[p, c],
                halo_recv.at[p, c],
                device_id=after,
                device_id_type=MESH,
            )
            halo.start()
            halos.append(halo)
        for c in range(WIDTH // 256):
            at = 2 * WIDTH + c * 256
            part = jnp.dot(inputs, w_ref[:, at : at + 256], preferred_element_type=jnp.float32)
            for s in range(2):
                at = c * 256 + s * pair
                q_ref[p, :, at : at + pair] = normalize_heads(
                    part[:, s * pair : (s + 1) * pair], all_low
                )
        attend_block(
            scale_ref,
            late,
            low,
            lambda p, l: q_ref[p, WINDOW:, l],
            lambda p, l: kv_ref[p, :WINDOW, l],
            lambda p, l: kv_ref[p, WINDOW:, l],
            p,
            att_ref,
            NY // 2,
            lambda c: None,
            lambda c: None,
        )
        give_back(p, NY // 2, NY, 0, WIDTH)
        attend_block(
            scale_ref,
            early,
            low,
            lambda p, l: q_ref[p, :WINDOW, l],
            lambda p, l: halo_ref[p, :, l],
            lambda p, l: kv_ref[p, :WINDOW, l],
            p,
            att_ref,
            0,
            lambda c: halos[c].wait(),
            lambda c: give_back(p, 0, NY // 2, c * pair, pair),
        )
    mine = pltpu.make_async_copy(att_ref.at[:, y], o_ref.at[y], own_sem.at[2 * frame_count + patches])
    mine.start()
    mine.wait()
    for f in range(frame_count):
        rest = slots_in_ref.at[f, pl.ds(0, n_he - 1)]
        pltpu.make_async_copy(rest, rest, slot_sem.at[0, f]).wait()
        pltpu.make_async_copy(rest, rest, part_sem.at[0, f]).wait()
    for p in range(patches):
        tokens_in = rows_ref.at[p, pl.ds(0, n - 1)]
        pltpu.make_async_copy(tokens_in, tokens_in, token_send.at[p]).wait()
    back = o_ref.at[pl.ds(0, NY - 1)]
    pltpu.make_async_copy(back, back, back_sem.at[1]).wait()
    pltpu.make_async_copy(back, back, back_sem.at[0]).wait()


def local(
    frame_patch_tokens,
    episode_first_frame,
    router,
    expert_up_weight,
    expert_down_weight,
    query_key_value_weight,
    head_score_scale,
):
    tokens = frame_patch_tokens.shape[2:]
    frame_count, patch_count, width = tokens
    n_ex = lax.axis_size("ex")
    n_half = lax.axis_size("half")
    n_he = n_half * n_ex
    n = NY * n_ex
    frames = n * frame_count
    span = frames // NY
    patches = patch_count // n
    groups = width // LANES
    slots = SPE * n_ex
    hidden = expert_up_weight.shape[2]
    starts = episode_first_frame.reshape(-1, WINDOW)
    vmem = pl.BlockSpec(memory_space=pltpu.VMEM)
    hbm = pl.BlockSpec(memory_space=pl.ANY)
    dma = pltpu.SemaphoreType.DMA

    def held(*shape):
        return pltpu.VMEM(shape, jnp.bfloat16)

    back = pl.pallas_call(
        functools.partial(whole_kernel, n_half, n_ex),
        out_shape=jax.ShapeDtypeStruct((NY, patches, span, WIDTH), jnp.bfloat16),
        in_specs=[pl.BlockSpec(memory_space=pltpu.SMEM), vmem] + [hbm] * 5,
        out_specs=vmem,
        scratch_shapes=[
            held(*tokens),
            held(*router.shape),
            held(frame_count, n_ex, SPE * groups, LANES),
            held(frame_count, n_he, SPE * groups, LANES),
            held(frame_count, n_he, SPE * groups, LANES),
            held(frame_count, n_he, SPE * groups, LANES),
            pltpu.VMEM((frame_count, patch_count, router.shape[1]), jnp.float32),
            held(patches, frame_count, n, groups, LANES),
            held(patches, n, frame_count, groups, LANES),
            pltpu.VMEM((frames * groups, LANES), jnp.float32),
            held(width, hidden),
            held(hidden, width),
            held(*query_key_value_weight.shape),
            held(patches, frames, WIDTH),
            held(patches, frames, 2 * WIDTH),
            held(patches, WINDOW, 2 * WIDTH),
            held(patches, NY, span, WIDTH),
            dma((5,)),
            dma((2 * frame_count + patches + 1,)),
            dma((2, frame_count)),
            dma((2, frame_count)),
            dma((patches,)),
            dma((patches,)),
            dma((patches, WIDTH // (2 * HEAD_SIZE))),
            dma((patches, WIDTH // (2 * HEAD_SIZE))),
            dma((2,)),
        ],
        compiler_params=pltpu.CompilerParams(collective_id=0, has_side_effects=True),
        name="whole",
    )(
        head_score_scale,
        starts,
        frame_patch_tokens,
        router,
        expert_up_weight,
        expert_down_weight,
        query_key_value_weight,
    )
    return back.transpose(2, 0, 1, 3).reshape(1, span, NY * patches, WIDTH)


def solution(mesh):
    placed = (
        P("half", "fr", "ex", None, None),
        P("half", None),
        P(),
        P("ex", None, "half"),
        P("ex", "half", None),
        P(),
        P(),
    )
    return jax.shard_map(
        local, mesh=mesh, in_specs=placed, out_specs=P("half", "fr", "ex", None), check_vma=False
    )
```

time: 98.5 us -> 93.1 us (0.945)
  the two profiles are of different devices: /device:TPU:44 before, /device:TPU:1 now
where the time goes in v4:
time: 93.1 us; the launch traced here: 92.9 us
  Pallas kernels  90.8 us (98%)
  local copies, waits for them, and re-layouts  2.13 us (2%)
    pallas_call x1, Pallas kernels, local(): pl.pallas_call(functools.partial(whole_kernel, n_half, n_ex), out_shape=j...  90.8 us
    reshape x1, local copies, waits for them, and re-layouts, local(): return back.transpose(2, 0, 1, 3).reshape(1, span, NY * patches, WIDTH)  2.13 us

profile of v4, /device:TPU:1, one launch (start us, length us, event | category | flops | bytes accessed | tf_op | source)
XLA Modules:
  0.0 92.9 jit_solution(14313662605373585658)
XLA Ops:
  0.0 90.8 %whole.1 = bf16[8,2,32,512]{3,2,1,0:T(8,128)(2,1)} custom-call(f32[8]{0:T(128)} %scale_ref.1, s32[8,128]{1,0:T(8,128)} %bitcast.5, bf16[1,1,2,256,1024]{4,3,2,1,0:T(8,128)(2,1)} %tok_hbm.1, bf16[1024,256]{1,0:T(8,128)(2,1)} %router_hbm.1, bf16[1,1024,1024]{2,1,0:T(8,128)(2,1)} %up_hbm.1, bf16[1,1024,1024]{2,1,0:T(8,128)(2,1)} %down_hbm.1, ...), custom_call_target="tpu_custom_call" | custom-call | tf_op jit(solution)/shard_map/whole/pallas_call | solution.py:482
  90.8 2.1 %copy.8 = bf16[1,32,16,512]{3,2,1,0:T(8,128)(2,1)} copy(bf16[1,32,16,512]{3,1,2,0:T(8,128)(2,1)} %bitcast.4) | data formatting | bytes 1048576 | tf_op jit(solution)/shard_map/reshape | solution.py:526
